TPU v7x, 32 devices: a whole 2x2x4 slice. The times are simulated.
32 devices in a mesh: rcp: 4 (over y, x), lon: 8 (over z, core).
Axes of the slice: x: 2, y: 2, z: 4, core: 2. Of those that a mesh axis runs over, the one named last changes fastest.
Arguments:
- adj_in: float32 [32, 32, 128, 128], P('rcp', None, 'lon'), may hold values from -6 to 6
- mass_flux: float32 [4, 2, 6, 32, 128, 128], P('rcp', None, None, None, 'lon'), may hold values from -0.24 to 0.24
- mixing: float32 [4, 128, 32, 32], P('rcp', 'lon'), may hold values from 0 to 0.7, as said below
- window_owner: int32 [6], replicated, may hold values from 0 to 3
- receptor_lon: int32 [32], P('rcp'), may hold values from 0 to 127
- receptor_lat: int32 [32], P('rcp'), may hold values from 0 to 127
- release_step: int32 [32], P('rcp'), may hold values from 0 to 5
Outputs:
- adj_out: float32 [32, 32, 128, 128], P('rcp', None, 'lon')
- footprint: float32 [32, 128, 128], P('rcp', 'lon')
Inputs may be any that keep to these rules, and one draw needn't show every extreme that they name: `mixing`: every entry is non-negative.
All inputs are finite; a program needn't handle non-finite values.
Results may differ from a plain program's by a relative error of at most 0.0003.
Values sent between devices are 32-bit elements; how exact they have to be, the bound alone decides.
No kernel may reach another device: no remote copies, remote signals or barrier semaphores. Data moves between devices by JAX's collectives and lax.ppermute only.
A program may use at most 128 MiB of HBM per device.

v0:
```python
import jax
import jax.numpy as jnp
from jax import lax
from jax.sharding import PartitionSpec as P

STEPS = 6


def from_root(block, axis, owner):
    block = jnp.where(lax.axis_index(axis) == owner, block, jnp.zeros_like(block))
    return lax.psum(block, axis)


def shifted(block, axis, distance):
    devices = range(lax.axis_size(axis))
    route = [((i - distance) % len(devices), i) for i in devices]
    return lax.ppermute(block, axis, route)


def padded_2(block, sides, width):
    for axis, dim in sides:
        count = lax.axis_size(axis)
        forward = [(i, i + 1) for i in range(count - 1)]
        forward.append((count - 1, 0))
        backward = [(target, source) for source, target in forward]
        low = lax.ppermute(
            lax.slice_in_dim(block, block.shape[dim] - width, None, axis=dim), axis, forward
        )
        high = lax.ppermute(lax.slice_in_dim(block, 0, width, axis=dim), axis, backward)
        block = jnp.concatenate([low, block, high], axis=dim)
    return block


def inject(field, columns, step, rlon, rlat, rel):
    lats = jnp.arange(field.shape[3], dtype=jnp.int32)
    hit = (
        (columns[None, :, None] == rlon[:, None, None])
        & (lats[None, None, :] == rlat[:, None, None])
        & (rel[:, None, None] == step)
    )
    return field.at[:, 0].add(hit.astype(jnp.float32))


def advance(padded, u_west, u_east, v_south, mats):
    centre = padded[:, :, 1:-1]
    left = padded[:, :, :-2]
    right = padded[:, :, 2:]
    west = jnp.maximum(u_west, 0.0) * left + jnp.minimum(u_west, 0.0) * centre
    east = jnp.maximum(u_east, 0.0) * centre + jnp.minimum(u_east, 0.0) * right
    lat_index = lax.broadcasted_iota(jnp.int32, v_south.shape, 2)
    vs = jnp.where(lat_index > 0, v_south, jnp.float32(0.0))
    vn = jnp.concatenate([vs[:, :, 1:], jnp.zeros_like(vs[:, :, :1])], axis=2)
    below = jnp.concatenate([jnp.zeros_like(centre[..., :1]), centre[..., :-1]], axis=3)
    above = jnp.concatenate([centre[..., 1:], jnp.zeros_like(centre[..., :1])], axis=3)
    south = jnp.maximum(vs, 0.0) * below + jnp.minimum(vs, 0.0) * centre
    north = jnp.maximum(vn, 0.0) * centre + jnp.minimum(vn, 0.0) * above
    moved = centre + west - east + south - north
    return jnp.einsum(
        "kab,rbky->raky",
        mats,
        moved,
        precision=lax.Precision.HIGHEST,
        preferred_element_type=jnp.float32,
    )


def local(adj_in, mass_flux, mixing, window_owner, receptor_lon, receptor_lat, release_step):
    flux_steps = []
    mat_steps = []
    for step in range(STEPS):
        flux_step, mats_step = (
            from_root(mass_flux[:, :, step], "rcp", window_owner[step]),
            from_root(mixing, "rcp", window_owner[step]),
        )
        flux_steps.append(flux_step[0])
        mat_steps.append(mats_step[0])
    flux = jnp.stack(flux_steps, axis=1)
    mats = jnp.stack(mat_steps, axis=0)
    width = adj_in.shape[2]
    start = lax.axis_index("lon") * width
    field = adj_in
    footprint = jnp.zeros((adj_in.shape[0], width, adj_in.shape[3]), jnp.float32)
    columns = start + jnp.arange(width, dtype=jnp.int32)
    edge = shifted(flux[0, :, :, 0:1, :], "lon", -1)
    east_all = jnp.concatenate([flux[0, :, :, 1:], edge], axis=2)
    for step in range(STEPS):
        field = inject(field, columns, step, receptor_lon, receptor_lat, release_step)
        padded = padded_2(field, (("lon", 2),), 1)
        field = advance(padded, flux[0, step], east_all[step], flux[1, step], mats[step])
        footprint = footprint + field[:, 0]
    return (field, footprint)


def solution(mesh):
    return jax.shard_map(
        local,
        mesh=mesh,
        in_specs=(
            P("rcp", None, "lon", None),
            P("rcp", None, None, None, "lon", None),
            P("rcp", "lon", None, None),
            P(),
            P("rcp"),
            P("rcp"),
            P("rcp"),
        ),
        out_specs=(P("rcp", None, "lon", None), P("rcp", "lon", None)),
        check_vma=False,
    )
```

profile of v0, /device:TPU:0, one launch (start us, length us, event | category | flops | bytes accessed | tf_op | source)
XLA Modules:
  0.0 259.4 jit_solution(11546297863126476404)
XLA Ops:
  7.2 1.6 fusion.231
  12.6 1.9 fusion.173
  14.5 3.3 %fusion.168 = (f32[1,2,32,16,128]{4,3,2,1,0:T(8,128)}, f32[1,2,32,16,128]{4,3,2,1,0:T(8,128)}, f32[1,2,32,16,128]{4,3,2,1,0:T(8,128)}, f32[1,2,32,16,128]{4,3,2,1,0:T(8,128)}, f32[1,2,32,16,128]{4,3,2,1,0:T(8,128)}) fusion(f32[1,2,6,32,16,128]{5,4,3,2,1,0:T(8,128)} %param.20, pred[]{:T(512)S(6)} %eq.64, pred[]{:T(512)S(6)} %eq.63, pred[]{:T(512)S(6)} %eq.61, ...), kind=kLoop, calls=%fused_computation.180 | loop fusion | flops 655360 | bytes 5242885 | tf_op jit(solution)/shard_map/jit(_where)/select_n | solution.py:10
  19.1 2.3 copy.62
  21.9 1.4 scatter-add.20
  24.5 4.0 %collective-permute-start.2 = (f32[8,32,1,128]{3,1,2,0:T(8,128)}, f32[8,32,1,128]{3,1,2,0:T(8,128)}, u32[]{:S(2)}, u32[]{:S(2)}) collective-permute-start(f32[8,32,1,128]{3,1,2,0:T(8,128)} %get-tuple-element.132), channel_id=1, source_target_pairs={{1,0},{2,1},{3,2},{4,3},{5,4},{6,5},{7,6},{0,7},{9,8},{10,9},{11,1... | collective-permute-start | bytes 393224 | tf_op jit(solution)/shard_map/ppermute | solution.py:29
  28.5 2.8 %fusion.229 = (f32[8,32,16,127]{3,1,2,0:T(8,128)}, f32[8,32,16,127]{3,1,2,0:T(8,128)}) fusion(f32[8,32,16,128]{3,1,2,0:T(8,128)S(1)} %scatter-add.20), kind=kLoop, calls=%fused_computation.333 | loop fusion | bytes 8323072 | tf_op jit(solution)/shard_map/slice | solution.py:53
  31.3 103.5 %all-reduce.21.cloned.1.call-done = (f32[1,2,32,16,128]{4,3,2,1,0:T(8,128)}, f32[1,2,32,16,128]{4,3,2,1,0:T(8,128)}, f32[1,2,32,16,128]{4,3,2,1,0:T(8,128)}, f32...) async-done(((f32[1,2,32,16,128]{4,3,2,1,0:T(8,128)}, ...) | async-done | bytes 3538960 | tf_op jit(solution)/shard_map/psum | solution.py:11
  140.2 2.8 %collective-permute-start.1 = (f32[6,32,1,128]{3,1,0,2:T(8,128)S(1)}, f32[6,32,1,128]{3,1,0,2:T(8,128)S(1)}, u32[]{:S(2)}, u32[]{:S(2)}) collective-permute-start(f32[6,32,1,128]{3,1,0,2:T(8,128)S(1)} %bitcast.219), channel_id=1, source_target_pairs={{1,0},{2,1},{3,2},{4,3},{5,4},{6,5},{7,6},{0,7},{9,8},{10,9},{11,1... | collective-permute-start | bytes 294920 | tf_op jit(solution)/shard_map/ppermute | solution.py:17
  170.1 4.4 %fusion.73 = f32[16,8,128,32]{2,3,1,0:T(8,128)S(1)} fusion(f32[16,32,32]{2,1,0:T(8,128)S(1)} %copy-done.60, f32[8,32,1,128]{3,1,2,0:T(8,128)} %collective-permute-done.2, f32[8,32,16,128]{3,1,2,0:T(8,128)S(1)} %scatter-add.20, f32[8,32,1,128]{3,1,2,0:T(8,128)} %collective-permute-done, f32[8,32,16,127]{3,1,2,0:T(8,128)S(1)} %copy-done.14, ...), kind=kOutput, calls=%fused_computation.80 | convolution fusion | flops 210763776 | bytes 10780672 | tf_op jit(solution)/shard_map/kab,rbky->raky/dot_general | solution.py:58
  176.6 2.0 scatter-add.21
  180.2 3.7 %collective-permute-start.4 = (f32[8,32,1,128]{3,1,0,2:T(8,128)S(1)}, f32[8,32,1,128]{3,1,0,2:T(8,128)S(1)}, u32[]{:S(2)}, u32[]{:S(2)}) collective-permute-start(f32[8,32,1,128]{3,1,0,2:T(8,128)S(1)} %get-tuple-element.128), channel_id=1, source_target_pairs={{1,0},{2,1},{3,2},{4,3},{5,4},{6,5},{7,6},{0,7},{9,8},{10,9},{11,1... | collective-permute-start | bytes 393224 | tf_op jit(solution)/shard_map/ppermute | solution.py:29
  187.8 3.4 %fusion.57 = f32[16,8,128,32]{2,3,1,0:T(8,128)S(1)} fusion(f32[8,32,1,128]{3,1,0,2:T(8,128)S(1)} %collective-permute-done.4, f32[8,32,16,128]{3,1,0,2:T(8,128)S(1)} %scatter-add.21, f32[8,32,1,128]{3,1,0,2:T(8,128)S(1)} %collective-permute-done.3, f32[8,32,16,127]{3,1,0,2:T(8,128)S(1)} %get-tuple-element.126, ...), kind=kOutput, calls=%fused_computation.63 | convolution fusion | flops 210763776 | bytes 10780672 | tf_op jit(solution)/shard_map/kab,rbky->raky/dot_general | solution.py:58
  192.7 1.4 scatter-add.24
  194.3 3.6 %collective-permute-start.6 = (f32[8,32,1,128]{3,1,0,2:T(8,128)S(1)}, f32[8,32,1,128]{3,1,0,2:T(8,128)S(1)}, u32[]{:S(2)}, u32[]{:S(2)}) collective-permute-start(f32[8,32,1,128]{3,1,0,2:T(8,128)S(1)} %get-tuple-element.124), channel_id=1, source_target_pairs={{1,0},{2,1},{3,2},{4,3},{5,4},{6,5},{7,6},{0,7},{9,8},{10,9},{11,1... | collective-permute-start | bytes 393224 | tf_op jit(solution)/shard_map/ppermute | solution.py:29
  198.5 2.8 %collective-permute-done.5 = f32[8,32,1,128]{3,1,0,2:T(8,128)S(1)} collective-permute-done((f32[8,32,1,128]{3,1,0,2:T(8,128)S(1)}, f32[8,32,1,128]{3,1,0,2:T(8,128)S(1)}, u32[]{:S(2)}, u32[]{:S(2)}) %collective-permute-start.5) | collective-permute-done | bytes 131104 | tf_op jit(solution)/shard_map/ppermute | solution.py:26
  201.5 3.4 %fusion.44 = f32[16,8,128,32]{2,3,1,0:T(8,128)S(1)} fusion(f32[8,32,1,128]{3,1,0,2:T(8,128)S(1)} %collective-permute-done.6, f32[8,32,16,128]{3,1,0,2:T(8,128)S(1)} %scatter-add.24, f32[8,32,1,128]{3,1,0,2:T(8,128)S(1)} %collective-permute-done.5, f32[8,32,16,127]{3,1,0,2:T(8,128)S(1)} %get-tuple-element.122, ...), kind=kOutput, calls=%fused_computation.50 | convolution fusion | flops 210763776 | bytes 10780672 | tf_op jit(solution)/shard_map/kab,rbky->raky/dot_general | solution.py:58
  206.4 1.4 scatter-add.25
  208.0 4.0 %collective-permute-start.8 = (f32[8,32,1,128]{3,1,0,2:T(8,128)S(1)}, f32[8,32,1,128]{3,1,0,2:T(8,128)S(1)}, u32[]{:S(2)}, u32[]{:S(2)}) collective-permute-start(f32[8,32,1,128]{3,1,0,2:T(8,128)S(1)} %get-tuple-element.120), channel_id=1, source_target_pairs={{1,0},{2,1},{3,2},{4,3},{5,4},{6,5},{7,6},{0,7},{9,8},{10,9},{11,1... | collective-permute-start | bytes 393224 | tf_op jit(solution)/shard_map/ppermute | solution.py:29
  212.7 2.5 collective-permute-done.7
  215.3 3.4 %fusion.31 = f32[16,8,128,32]{2,3,1,0:T(8,128)S(1)} fusion(f32[8,32,1,128]{3,1,0,2:T(8,128)S(1)} %collective-permute-done.8, f32[8,32,16,128]{3,1,0,2:T(8,128)S(1)} %scatter-add.25, f32[8,32,1,128]{3,1,0,2:T(8,128)S(1)} %collective-permute-done.7, f32[8,32,16,127]{3,1,0,2:T(8,128)S(1)} %get-tuple-element.118, ...), kind=kOutput, calls=%fused_computation.37 | convolution fusion | flops 210763776 | bytes 10780672 | tf_op jit(solution)/shard_map/kab,rbky->raky/dot_general | solution.py:58
  220.3 1.4 scatter-add.26
  221.7 3.0 %collective-permute-start.10 = (f32[8,32,1,128]{3,1,0,2:T(8,128)S(1)}, f32[8,32,1,128]{3,1,0,2:T(8,128)S(1)}, u32[]{:S(2)}, u32[]{:S(2)}) collective-permute-start(f32[8,32,1,128]{3,1,0,2:T(8,128)S(1)} %get-tuple-element.116), channel_id=1, source_target_pairs={{1,0},{2,1},{3,2},{4,3},{5,4},{6,5},{7,6},{0,7},{9,8},{10,9},{11,1... | collective-permute-start | bytes 393224 | tf_op jit(solution)/shard_map/ppermute | solution.py:29
  225.5 1.7 collective-permute-done.10
  227.2 3.8 %collective-permute-done.9 = f32[8,32,1,128]{3,1,0,2:T(8,128)S(1)} collective-permute-done((f32[8,32,1,128]{3,1,0,2:T(8,128)S(1)}, f32[8,32,1,128]{3,1,0,2:T(8,128)S(1)}, u32[]{:S(2)}, u32[]{:S(2)}) %collective-permute-start.9) | collective-permute-done | bytes 131104 | tf_op jit(solution)/shard_map/ppermute | solution.py:26
  231.0 3.4 %fusion.18 = f32[16,8,128,32]{2,3,1,0:T(8,128)S(1)} fusion(f32[8,32,1,128]{3,1,0,2:T(8,128)S(1)} %collective-permute-done.10, f32[8,32,16,128]{3,1,0,2:T(8,128)S(1)} %scatter-add.26, f32[8,32,1,128]{3,1,0,2:T(8,128)S(1)} %collective-permute-done.9, f32[8,32,16,127]{3,1,0,2:T(8,128)S(1)} %get-tuple-element.114, ...), kind=kOutput, calls=%fused_computation.24 | convolution fusion | flops 210763776 | bytes 10780672 | tf_op jit(solution)/shard_map/kab,rbky->raky/dot_general | solution.py:58
  236.0 1.4 scatter-add.29
  237.5 3.7 %collective-permute-start.12 = (f32[8,32,1,128]{3,1,0,2:T(8,128)S(1)}, f32[8,32,1,128]{3,1,0,2:T(8,128)S(1)}, u32[]{:S(2)}, u32[]{:S(2)}) collective-permute-start(f32[8,32,1,128]{3,1,0,2:T(8,128)S(1)} %get-tuple-element.112), channel_id=1, source_target_pairs={{1,0},{2,1},{3,2},{4,3},{5,4},{6,5},{7,6},{0,7},{9,8},{10,9},{11,1... | collective-permute-start | bytes 393224 | tf_op jit(solution)/shard_map/ppermute | solution.py:29
  241.9 1.7 collective-permute-done.11
  243.8 3.4 %fusion.125 = f32[8,32,16,128]{3,1,0,2:T(8,128)S(1)} fusion(f32[8,32,1,128]{3,1,0,2:T(8,128)S(1)} %collective-permute-done.12, f32[8,32,16,128]{3,1,0,2:T(8,128)S(1)} %scatter-add.29, f32[8,32,1,128]{3,1,0,2:T(8,128)S(1)} %collective-permute-done.11, f32[8,32,16,127]{3,1,0,2:T(8,128)S(1)} %get-tuple-element.110, ...), kind=kOutput, calls=%fused_computation.132 | convolution fusion | flops 210763776 | bytes 10780672 | tf_op jit(solution)/shard_map/kab,rbky->raky/dot_general | solution.py:58
  247.2 2.0 slice_add_fusion
  249.2 2.5 copy.120
  (253 shorter events, 52.7 us)
Async XLA Ops:
  7.2 127.7 %all-reduce.21.cloned.1.call-start = ((), (), s32[]{:S(2)}) async-start(), calls=%async_computation | async-start | bytes 9437184 | tf_op jit(solution)/shard_map/psum | solution.py:11
  24.0 144.9 %collective-permute-start = (f32[8,32,1,128]{3,1,2,0:T(8,128)}, f32[8,32,1,128]{3,1,2,0:T(8,128)}, u32[]{:S(2)}, u32[]{:S(2)}) collective-permute-start(f32[8,32,1,128]{3,1,2,0:T(8,128)} %get-tuple-element.131), channel_id=1, source_target_pairs={{0,1},{1,2},{2,3},{3,4},{4,5},{5,6},{6,7},{7,0},{8,9},{9,10},{10,1... | collective-permute-start | bytes 393224 | tf_op jit(solution)/shard_map/ppermute | solution.py:26
  24.5 144.4 %collective-permute-start.2 = (f32[8,32,1,128]{3,1,2,0:T(8,128)}, f32[8,32,1,128]{3,1,2,0:T(8,128)}, u32[]{:S(2)}, u32[]{:S(2)}) collective-permute-start(f32[8,32,1,128]{3,1,2,0:T(8,128)} %get-tuple-element.132), channel_id=1, source_target_pairs={{1,0},{2,1},{3,2},{4,3},{5,4},{6,5},{7,6},{0,7},{9,8},{10,9},{11,1... | collective-permute-start | bytes 393224 | tf_op jit(solution)/shard_map/ppermute | solution.py:29
  137.6 30.0 %copy-start = (f32[6,32,15,128]{3,2,1,0:T(8,128)}, f32[6,32,15,128]{3,2,1,0:T(8,128)S(1)}, u32[]{:S(2)}) copy-start(f32[6,32,15,128]{3,2,1,0:T(8,128)S(1)} %slice_bitcast_fusion) | copy-start | bytes 4423684
  140.2 27.3 %collective-permute-start.1 = (f32[6,32,1,128]{3,1,0,2:T(8,128)S(1)}, f32[6,32,1,128]{3,1,0,2:T(8,128)S(1)}, u32[]{:S(2)}, u32[]{:S(2)}) collective-permute-start(f32[6,32,1,128]{3,1,0,2:T(8,128)S(1)} %bitcast.219), channel_id=1, source_target_pairs={{1,0},{2,1},{3,2},{4,3},{5,4},{6,5},{7,6},{0,7},{9,8},{10,9},{11,1... | collective-permute-start | bytes 294920 | tf_op jit(solution)/shard_map/ppermute | solution.py:17
  180.1 7.6 %collective-permute-start.3 = (f32[8,32,1,128]{3,1,0,2:T(8,128)S(1)}, f32[8,32,1,128]{3,1,0,2:T(8,128)S(1)}, u32[]{:S(2)}, u32[]{:S(2)}) collective-permute-start(f32[8,32,1,128]{3,1,0,2:T(8,128)S(1)} %get-tuple-element.127), channel_id=1, source_target_pairs={{0,1},{1,2},{2,3},{3,4},{4,5},{5,6},{6,7},{7,0},{8,9},{9,10},{10,1... | collective-permute-start | bytes 393224 | tf_op jit(solution)/shard_map/ppermute | solution.py:26
  180.2 7.5 %collective-permute-start.4 = (f32[8,32,1,128]{3,1,0,2:T(8,128)S(1)}, f32[8,32,1,128]{3,1,0,2:T(8,128)S(1)}, u32[]{:S(2)}, u32[]{:S(2)}) collective-permute-start(f32[8,32,1,128]{3,1,0,2:T(8,128)S(1)} %get-tuple-element.128), channel_id=1, source_target_pairs={{1,0},{2,1},{3,2},{4,3},{5,4},{6,5},{7,6},{0,7},{9,8},{10,9},{11,1... | collective-permute-start | bytes 393224 | tf_op jit(solution)/shard_map/ppermute | solution.py:29
  194.1 7.3 %collective-permute-start.5 = (f32[8,32,1,128]{3,1,0,2:T(8,128)S(1)}, f32[8,32,1,128]{3,1,0,2:T(8,128)S(1)}, u32[]{:S(2)}, u32[]{:S(2)}) collective-permute-start(f32[8,32,1,128]{3,1,0,2:T(8,128)S(1)} %get-tuple-element.123), channel_id=1, source_target_pairs={{0,1},{1,2},{2,3},{3,4},{4,5},{5,6},{6,7},{7,0},{8,9},{9,10},{10,1... | collective-permute-start | bytes 393224 | tf_op jit(solution)/shard_map/ppermute | solution.py:26
  194.2 7.2 %copy-start.36 = (f32[32,16,128]{2,0,1:T(8,128)S(1)}, f32[32,16,128]{2,0,1:T(8,128)}, u32[]{:S(2)}) copy-start(f32[32,16,128]{2,0,1:T(8,128)} %copy.94) | copy-start | bytes 786436
  194.2 7.2 %copy-start.37 = (f32[32,16,128]{2,0,1:T(8,128)S(1)}, f32[32,16,128]{2,0,1:T(8,128)}, u32[]{:S(2)}) copy-start(f32[32,16,128]{2,0,1:T(8,128)} %copy.95) | copy-start | bytes 786436
  194.2 7.2 %copy-start.38 = (f32[32,16,128]{2,0,1:T(8,128)S(1)}, f32[32,16,128]{2,0,1:T(8,128)}, u32[]{:S(2)}) copy-start(f32[32,16,128]{2,0,1:T(8,128)} %copy.93) | copy-start | bytes 786436
  194.2 7.2 %copy-start.39 = (f32[32,16,128]{2,0,1:T(8,128)S(1)}, f32[32,16,128]{2,0,1:T(8,128)}, u32[]{:S(2)}) copy-start(f32[32,16,128]{2,0,1:T(8,128)} %copy.92) | copy-start | bytes 786436
  194.2 7.2 %copy-start.40 = (f32[32,16,128]{2,0,1:T(8,128)S(1)}, f32[32,16,128]{2,0,1:T(8,128)}, u32[]{:S(2)}) copy-start(f32[32,16,128]{2,0,1:T(8,128)} %copy.88) | copy-start | bytes 786436
  194.2 7.2 %copy-start.41 = (f32[32,16,128]{2,0,1:T(8,128)S(1)}, f32[32,16,128]{2,0,1:T(8,128)}, u32[]{:S(2)}) copy-start(f32[32,16,128]{2,0,1:T(8,128)} %copy.89) | copy-start | bytes 786436
  194.2 7.2 %copy-start.50 = (f32[32,16,128]{2,0,1:T(8,128)S(1)}, f32[32,16,128]{2,0,1:T(8,128)}, u32[]{:S(2)}) copy-start(f32[32,16,128]{2,0,1:T(8,128)} %copy.90) | copy-start | bytes 786436
  194.2 7.2 %copy-start.51 = (f32[32,16,128]{2,0,1:T(8,128)S(1)}, f32[32,16,128]{2,0,1:T(8,128)}, u32[]{:S(2)}) copy-start(f32[32,16,128]{2,0,1:T(8,128)} %copy.91) | copy-start | bytes 786436
  194.3 7.1 %collective-permute-start.6 = (f32[8,32,1,128]{3,1,0,2:T(8,128)S(1)}, f32[8,32,1,128]{3,1,0,2:T(8,128)S(1)}, u32[]{:S(2)}, u32[]{:S(2)}) collective-permute-start(f32[8,32,1,128]{3,1,0,2:T(8,128)S(1)} %get-tuple-element.124), channel_id=1, source_target_pairs={{1,0},{2,1},{3,2},{4,3},{5,4},{6,5},{7,6},{0,7},{9,8},{10,9},{11,1... | collective-permute-start | bytes 393224 | tf_op jit(solution)/shard_map/ppermute | solution.py:29
  207.8 7.4 %collective-permute-start.7 = (f32[8,32,1,128]{3,1,0,2:T(8,128)S(1)}, f32[8,32,1,128]{3,1,0,2:T(8,128)S(1)}, u32[]{:S(2)}, u32[]{:S(2)}) collective-permute-start(f32[8,32,1,128]{3,1,0,2:T(8,128)S(1)} %get-tuple-element.119), channel_id=1, source_target_pairs={{0,1},{1,2},{2,3},{3,4},{4,5},{5,6},{6,7},{7,0},{8,9},{9,10},{10,1... | collective-permute-start | bytes 393224 | tf_op jit(solution)/shard_map/ppermute | solution.py:26
  207.9 7.3 %copy-start.30 = (f32[32,16,128]{2,0,1:T(8,128)S(1)}, f32[32,16,128]{2,0,1:T(8,128)}, u32[]{:S(2)}) copy-start(f32[32,16,128]{2,0,1:T(8,128)} %copy.102) | copy-start | bytes 786436
  207.9 7.3 %copy-start.31 = (f32[32,16,128]{2,0,1:T(8,128)S(1)}, f32[32,16,128]{2,0,1:T(8,128)}, u32[]{:S(2)}) copy-start(f32[32,16,128]{2,0,1:T(8,128)} %copy.103) | copy-start | bytes 786436
  207.9 7.3 %copy-start.32 = (f32[32,16,128]{2,0,1:T(8,128)S(1)}, f32[32,16,128]{2,0,1:T(8,128)}, u32[]{:S(2)}) copy-start(f32[32,16,128]{2,0,1:T(8,128)} %copy.101) | copy-start | bytes 786436
  207.9 7.3 %copy-start.33 = (f32[32,16,128]{2,0,1:T(8,128)S(1)}, f32[32,16,128]{2,0,1:T(8,128)}, u32[]{:S(2)}) copy-start(f32[32,16,128]{2,0,1:T(8,128)} %copy.100) | copy-start | bytes 786436
  207.9 7.3 %copy-start.34 = (f32[32,16,128]{2,0,1:T(8,128)S(1)}, f32[32,16,128]{2,0,1:T(8,128)}, u32[]{:S(2)}) copy-start(f32[32,16,128]{2,0,1:T(8,128)} %copy.96) | copy-start | bytes 786436
  207.9 7.3 %copy-start.35 = (f32[32,16,128]{2,0,1:T(8,128)S(1)}, f32[32,16,128]{2,0,1:T(8,128)}, u32[]{:S(2)}) copy-start(f32[32,16,128]{2,0,1:T(8,128)} %copy.97) | copy-start | bytes 786436
  207.9 7.3 %copy-start.48 = (f32[32,16,128]{2,0,1:T(8,128)S(1)}, f32[32,16,128]{2,0,1:T(8,128)}, u32[]{:S(2)}) copy-start(f32[32,16,128]{2,0,1:T(8,128)} %copy.98) | copy-start | bytes 786436
  208.0 7.3 %copy-start.49 = (f32[32,16,128]{2,0,1:T(8,128)S(1)}, f32[32,16,128]{2,0,1:T(8,128)}, u32[]{:S(2)}) copy-start(f32[32,16,128]{2,0,1:T(8,128)} %copy.99) | copy-start | bytes 786436
  208.0 7.3 %copy-start.57 = (f32[16,32,32]{2,1,0:T(8,128)S(1)}, f32[16,32,32]{2,1,0:T(8,128)}, u32[]{:S(2)}) copy-start(f32[16,32,32]{2,1,0:T(8,128)} %get-tuple-element.87) | copy-start | bytes 196612
  208.0 7.2 %collective-permute-start.8 = (f32[8,32,1,128]{3,1,0,2:T(8,128)S(1)}, f32[8,32,1,128]{3,1,0,2:T(8,128)S(1)}, u32[]{:S(2)}, u32[]{:S(2)}) collective-permute-start(f32[8,32,1,128]{3,1,0,2:T(8,128)S(1)} %get-tuple-element.120), channel_id=1, source_target_pairs={{1,0},{2,1},{3,2},{4,3},{5,4},{6,5},{7,6},{0,7},{9,8},{10,9},{11,1... | collective-permute-start | bytes 393224 | tf_op jit(solution)/shard_map/ppermute | solution.py:29
  221.7 5.5 %collective-permute-start.10 = (f32[8,32,1,128]{3,1,0,2:T(8,128)S(1)}, f32[8,32,1,128]{3,1,0,2:T(8,128)S(1)}, u32[]{:S(2)}, u32[]{:S(2)}) collective-permute-start(f32[8,32,1,128]{3,1,0,2:T(8,128)S(1)} %get-tuple-element.116), channel_id=1, source_target_pairs={{1,0},{2,1},{3,2},{4,3},{5,4},{6,5},{7,6},{0,7},{9,8},{10,9},{11,1... | collective-permute-start | bytes 393224 | tf_op jit(solution)/shard_map/ppermute | solution.py:29
  224.7 6.2 %collective-permute-start.9 = (f32[8,32,1,128]{3,1,0,2:T(8,128)S(1)}, f32[8,32,1,128]{3,1,0,2:T(8,128)S(1)}, u32[]{:S(2)}, u32[]{:S(2)}) collective-permute-start(f32[8,32,1,128]{3,1,0,2:T(8,128)S(1)} %get-tuple-element.115), channel_id=1, source_target_pairs={{0,1},{1,2},{2,3},{3,4},{4,5},{5,6},{6,7},{7,0},{8,9},{9,10},{10,1... | collective-permute-start | bytes 393224 | tf_op jit(solution)/shard_map/ppermute | solution.py:26
  237.4 6.2 %collective-permute-start.11 = (f32[8,32,1,128]{3,1,0,2:T(8,128)S(1)}, f32[8,32,1,128]{3,1,0,2:T(8,128)S(1)}, u32[]{:S(2)}, u32[]{:S(2)}) collective-permute-start(f32[8,32,1,128]{3,1,0,2:T(8,128)S(1)} %get-tuple-element.111), channel_id=1, source_target_pairs={{0,1},{1,2},{2,3},{3,4},{4,5},{5,6},{6,7},{7,0},{8,9},{9,10},{10,1... | collective-permute-start | bytes 393224 | tf_op jit(solution)/shard_map/ppermute | solution.py:26
  237.5 6.2 %collective-permute-start.12 = (f32[8,32,1,128]{3,1,0,2:T(8,128)S(1)}, f32[8,32,1,128]{3,1,0,2:T(8,128)S(1)}, u32[]{:S(2)}, u32[]{:S(2)}) collective-permute-start(f32[8,32,1,128]{3,1,0,2:T(8,128)S(1)} %get-tuple-element.112), channel_id=1, source_target_pairs={{1,0},{2,1},{3,2},{4,3},{5,4},{6,5},{7,6},{0,7},{9,8},{10,9},{11,1... | collective-permute-start | bytes 393224 | tf_op jit(solution)/shard_map/ppermute | solution.py:29
  (45 other events, 168.2 us)
Sparse Core Ops, SparseCore 0:
  19.2 115.5 all-reduce.20
where the time goes:
time: 264 us; the launch traced here: 259 us
  waiting for transfers between devices  116 us (44%)
  local copies, waits for them, and re-layouts  64.2 us (24%)
  starting transfers between devices  25.6 us (10%)
  matrix products  21.3 us (8%)
  between operations  19.4 us (7%)
  other arithmetic  12.6 us (5%)
    psum x1, waiting for transfers between devices, from_root(): return lax.psum(block, axis)  103 us
    ppermute x6, starting transfers between devices, padded_2(): lax.ppermute(lax.slice_in_dim(block, 0, width, axis=dim), axis, backward)  22 us
    dot_general x6, matrix products, advance(): jnp.einsum('kab,rbky->raky', mats, moved, precision=lax.Precision.HIGHEST...  21.3 us
    unnamed x137, local copies, waits for them, and re-layouts  17.6 us
    ppermute x6, waiting for transfers between devices, padded_2(): lax.ppermute(lax.slice_in_dim(block, block.shape[dim] - width, None, axis...  10.8 us
    scatter-add x6, local copies, waits for them, and re-layouts, inject(): return field.at[:, 0].add(hit.astype(jnp.float32))  8.81 us
    slice x6, local copies, waits for them, and re-layouts, advance(): centre[..., :-1]  6.41 us
  transfers between devices with their start and end apart: 14, of which 7 were waited for; matrix products, arithmetic and copies ran while one was open for 17% of the time, Pallas kernels for 0%

commit v1 on v0

v1 whole, which is shorter than its diff:
```python
import functools

import jax
import jax.numpy as jnp
from jax import lax
from jax.experimental import pallas as pl
from jax.experimental.pallas import tpu as pltpu
from jax.sharding import PartitionSpec as P

CHUNKS = ((0, 1, 2), (3, 4), (5,))


def flip(block, bit):
    count = lax.axis_size("rcp")
    return lax.ppermute(block, "rcp", [(i, i ^ (1 << bit)) for i in range(count)])


def along(block, distance):
    count = lax.axis_size("lon")
    return lax.ppermute(block, "lon", [(i, (i + distance) % count) for i in range(count)])


def from_owner(block, owners, order):
    count = lax.axis_size("rcp")
    if count & (count - 1) or block.shape[1] % count:
        mine = owners == lax.axis_index("rcp")
        return lax.psum(jnp.where(mine[:, None, None, None], block, 0.0), "rcp")
    me = lax.axis_index("rcp")
    for bit in order:
        side = (me >> bit) & 1
        half = block.shape[1] // 2
        send = lax.dynamic_slice_in_dim(block, (1 - side) * half, half, axis=1)
        keep = lax.dynamic_slice_in_dim(block, side * half, half, axis=1)
        got = flip(send, bit)
        same = ((owners >> bit) & 1) == side
        block = jnp.where(same[:, None, None, None], keep, got)
    for bit in order[::-1]:
        side = (me >> bit) & 1
        got = flip(block, bit)
        block = jnp.where(
            side == 0,
            jnp.concatenate([block, got], axis=1),
            jnp.concatenate([got, block], axis=1),
        )
    return block


def gather_slots(block):
    count = lax.axis_size("rcp")
    if count & (count - 1):
        return lax.all_gather(block, "rcp", axis=0, tiled=True)
    me = lax.axis_index("rcp")
    for bit in range(count.bit_length() - 1):
        side = (me >> bit) & 1
        got = flip(block, bit)
        block = jnp.where(
            side == 0,
            jnp.concatenate([block, got], axis=0),
            jnp.concatenate([got, block], axis=0),
        )
    return block


def steps_kernel(steps, total, reach, owner_ref, rlon_ref, rlat_ref, rel_ref, start_ref,
                 field_hbm, foot_ref, u_ref, v_ref, mats_ref, out_ref, foot_out_ref,
                 field_ref, other_ref, sem):
    count, ext, lev, lat = field_ref.shape
    halo = total
    width = ext - 2 * halo
    nlon = width * lax.axis_size("lon")
    load = pltpu.make_async_copy(field_hbm, field_ref, sem)
    load.start()
    foot_out_ref[...] = foot_ref[...]
    lane = lax.broadcasted_iota(jnp.int32, (lev, lat), 1)
    lane_row = lax.broadcasted_iota(jnp.int32, (1, lat), 1)
    first = lane == 0
    last = lane == lat - 1

    load.wait()
    bufs = [(field_ref, other_ref)[k % 2] for k in range(len(steps))] + [out_ref]
    for k, step in enumerate(steps):
        src, dst = bufs[k], bufs[k + 1]
        owner = owner_ref[step]
        for r in range(count):
            col = lax.rem(rlon_ref[r] - start_ref[0] + halo + nlon, nlon)

            @pl.when((rel_ref[r] == step) & (col < ext))
            def _():
                row = src[r, pl.ds(col, 1), 0:1, :]
                src[r, pl.ds(col, 1), 0:1, :] = row + jnp.where(
                    lane_row == rlat_ref[r], 1.0, 0.0
                )[None]

        def column(c, carry, src=src, dst=dst, k=k, owner=owner):
            j = c - halo + reach
            uw = u_ref[k, j]
            ue = u_ref[k, j + 1]
            vs = jnp.where(first, 0.0, v_ref[k, j])
            vn = jnp.where(last, 0.0, pltpu.roll(v_ref[k, j], lat - 1, 1))
            cw = jnp.maximum(uw, 0.0)
            ce = -jnp.minimum(ue, 0.0)
            cs = jnp.maximum(vs, 0.0)
            cn = -jnp.minimum(vn, 0.0)
            c0 = 1.0 + (jnp.minimum(uw, 0.0) - jnp.maximum(ue, 0.0)) + (
                jnp.minimum(vs, 0.0) - jnp.maximum(vn, 0.0)
            )
            his, los = [], []
            for r in range(count):
                q = src[r, c]
                p = c0 * q + cw * src[r, c - 1] + ce * src[r, c + 1]
                p = p + cs * pltpu.roll(q, 1, 1) + cn * pltpu.roll(q, lat - 1, 1)
                hi = p.astype(jnp.bfloat16)
                his.append(hi)
                los.append((p - hi.astype(jnp.float32)).astype(jnp.bfloat16))
            hi = jnp.concatenate(his, axis=1)
            lo = jnp.concatenate(los, axis=1)
            new = jnp.dot(
                mats_ref[owner * ext + c],
                jnp.concatenate([hi, lo, hi], axis=0),
                preferred_element_type=jnp.float32,
            )
            for r in range(count):
                dst[r, c] = new[:, r * lat:(r + 1) * lat]

            @pl.when((c >= halo) & (c < halo + width))
            def _():
                for r in range(count):
                    row = foot_out_ref[r, pl.ds(c - halo, 1), :]
                    foot_out_ref[r, pl.ds(c - halo, 1), :] = row + new[0:1, r * lat:(r + 1) * lat]

            return carry

        lax.fori_loop(step + 1, ext - step - 1, column, 0)


def run_steps(steps, total, reach, scalars, field, foot, u, v, mats):
    smem = pl.BlockSpec(memory_space=pltpu.SMEM)
    vmem = pl.BlockSpec(memory_space=pltpu.VMEM)
    return pl.pallas_call(
        functools.partial(steps_kernel, steps, total, reach),
        out_shape=(
            jax.ShapeDtypeStruct(field.shape, jnp.float32),
            jax.ShapeDtypeStruct(foot.shape, jnp.float32),
        ),
        in_specs=[smem] * 5 + [pl.BlockSpec(memory_space=pl.ANY)] + [vmem] * 4,
        out_specs=(vmem, vmem),
        scratch_shapes=[pltpu.VMEM(field.shape, jnp.float32)] * 2 + [pltpu.SemaphoreType.DMA],
        compiler_params=pltpu.CompilerParams(vmem_limit_bytes=48 << 20),
        cost_estimate=pl.CostEstimate(
            flops=int(len(steps) * field.size * 200), bytes_accessed=int(field.size * 8),
            transcendentals=0,
        ),
        name="steps_%d" % steps[0],
    )(*scalars, field, foot, u, v, mats)


def local(adj_in, mass_flux, mixing, window_owner, receptor_lon, receptor_lat, release_step):
    count, lev, width, lat = adj_in.shape
    total = mass_flux.shape[2]
    start = (lax.axis_index("lon") * width).astype(jnp.int32)[None]
    scalars = (window_owner, receptor_lon, receptor_lat, release_step, start)
    bits = tuple(range((lax.axis_size("rcp") - 1).bit_length()))

    field = adj_in.transpose(0, 2, 1, 3)
    west = along(field[:, width - total:], 1)
    east = along(field[:, :total], -1)
    field = jnp.concatenate([west, field, east], axis=1)
    ext = width + 2 * total

    mats = mixing[0]
    mats_west = along(mats[width - total:], 1)
    mats_east = along(mats[:total], -1)
    mats = jnp.concatenate([mats_west, mats, mats_east], axis=0)
    pack = lat // lev
    mats = mats.reshape(ext // pack, pack, lev, lev).transpose(0, 2, 1, 3)
    mats = gather_slots(mats.reshape(1, ext // pack, lev, pack * lev))
    slots = mats.shape[0]
    mats = mats.reshape(slots, ext // pack, lev, pack, lev).transpose(0, 1, 3, 2, 4)
    mats = mats.reshape(slots * ext, lev, lev)
    high = lax.reduce_precision(mats, exponent_bits=8, mantissa_bits=7)
    mats = jnp.concatenate([high, high, mats - high], axis=2).astype(jnp.bfloat16)

    flux = mass_flux[0].transpose(0, 1, 3, 2, 4)
    foot = jnp.zeros((count, width, lat), jnp.float32)
    for steps in CHUNKS:
        reach = total - 1 - steps[0]
        owners = jnp.stack([window_owner[s] for s in steps])
        rows = slice(steps[0], steps[-1] + 1)
        u = from_owner(flux[0, rows], owners, bits)
        v = from_owner(flux[1, rows], owners, bits[::-1])
        right = along(u[:, :reach + 1] if reach == 0 else jnp.concatenate([u[:, :reach + 1], v[:, :reach]], axis=1), -1)
        if reach:
            left = along(jnp.concatenate([u[:, width - reach:], v[:, width - reach:]], axis=1), 1)
            u = jnp.concatenate([left[:, :reach], u, right[:, :reach + 1]], axis=1)
            v = jnp.concatenate([left[:, reach:], v, right[:, reach + 1:]], axis=1)
        else:
            u = jnp.concatenate([u, right], axis=1)
        field, foot = run_steps(steps, total, reach, scalars, field, foot, u, v, mats)
    return field[:, total:total + width].transpose(0, 2, 1, 3), foot


def solution(mesh):
    return jax.shard_map(
        local,
        mesh=mesh,
        in_specs=(
            P("rcp", None, "lon", None),
            P("rcp", None, None, None, "lon", None),
            P("rcp", "lon", None, None),
            P(),
            P("rcp"),
            P("rcp"),
            P("rcp"),
        ),
        out_specs=(P("rcp", None, "lon", None), P("rcp", "lon", None)),
        check_vma=False,
    )
```

time: 264 us -> 195 us (0.74)
  waiting for transfers between devices: 116 us -> 51.1 us
  Pallas kernels: 0 us -> 45.8 us
  local copies, waits for them, and re-layouts: 64.2 us -> 30.1 us
  matrix products: 21.3 us -> 0 us
  starting transfers between devices: 25.6 us -> 44.5 us
  between operations: 19.4 us -> 2.75 us
  other arithmetic: 12.6 us -> 18.1 us
    psum x1 -> x0, waiting for transfers between devices: 103 us -> none  [from_root(): return lax.psum(block, axis)]
    pallas_call x0 -> x3, Pallas kernels: none -> 45.8 us  [run_steps(): pl.pallas_call(functools.partial(steps_kernel, steps, total, reach), out_...]
    ppermute x13 -> x35, waiting for transfers between devices: 12.6 us -> 51.1 us  [the longest x26 39.1 us: flip(): return lax.ppermute(block, 'rcp', [(i, i ^ 1 << bit) for i in range(count)])]
    dot_general x6 -> x0, matrix products: 21.3 us -> none  [advance(): jnp.einsum('kab,rbky->raky', mats, moved, precision=lax.Precision.HIGHEST...]
    ppermute x13 -> x35, starting transfers between devices: 25.6 us -> 44.5 us  [the longest x26 27.8 us: flip(): return lax.ppermute(block, 'rcp', [(i, i ^ 1 << bit) for i in range(count)])]
    max x18 -> x0, local copies, waits for them, and re-layouts: 12.1 us -> none  [the longest x6 4.05 us: advance(): north = jnp.maximum(vn, 0.0) * centre + jnp.minimum(vn, 0.0) * above]
    min x18 -> x0, local copies, waits for them, and re-layouts: 12 us -> none  [the longest x6 4.02 us: advance(): south = jnp.maximum(vs, 0.0) * below + jnp.minimum(vs, 0.0) * centre]
    dynamic_slice x0 -> x15, local copies, waits for them, and re-layouts: none -> 9.82 us  [the longest x12 7.29 us: from_owner(): send = lax.dynamic_slice_in_dim(block, (1 - side) * half, half, axis=1)]
  transfers between devices with their start and end apart: 14 -> 35, of which waited for: 7 -> 17; matrix products, arithmetic and copies ran while one was open for 17% -> 19% of each run, Pallas kernels for 0% -> 0%
where the time goes in v1:
time: 195 us; the launch traced here: 192 us
  waiting for transfers between devices  51.1 us (26%)
  Pallas kernels  45.8 us (23%)
  starting transfers between devices  44.5 us (23%)
  local copies, waits for them, and re-layouts  30.1 us (15%)
  other arithmetic  18.1 us (9%)
  between operations  2.75 us (1%)
    pallas_call x3, Pallas kernels, run_steps(): pl.pallas_call(functools.partial(steps_kernel, steps, total, reach), out_...  45.8 us
    ppermute x26, waiting for transfers between devices, flip(): return lax.ppermute(block, 'rcp', [(i, i ^ 1 << bit) for i in range(count)])  39.1 us
    ppermute x26, starting transfers between devices, flip(): return lax.ppermute(block, 'rcp', [(i, i ^ 1 << bit) for i in range(count)])  27.8 us
    ppermute x9, starting transfers between devices, along(): lax.ppermute(block, 'lon', [(i, (i + distance) % count) for i in range(co...  16.8 us
    ppermute x9, waiting for transfers between devices, along(): lax.ppermute(block, 'lon', [(i, (i + distance) % count) for i in range(co...  12.1 us
    unnamed x64, local copies, waits for them, and re-layouts  9.55 us
    select_n x12, other arithmetic, from_owner(): block = jnp.where(same[:, None, None, None], keep, got)  7.4 us
    dynamic_slice x12, local copies, waits for them, and re-layouts, from_owner(): send = lax.dynamic_slice_in_dim(block, (1 - side) * half, half, axis=1)  7.29 us
  transfers between devices with their start and end apart: 35, of which 17 were waited for; matrix products, arithmetic and copies ran while one was open for 19% of the time, Pallas kernels for 0%

profile of v1, /device:TPU:0, one launch (start us, length us, event | category | flops | bytes accessed | tf_op | source)
XLA Modules:
  0.0 192.4 jit_solution(14176266973178546861)
XLA Ops:
  0.6 2.2 %copy.70 = f32[8,32,16,128]{3,1,2,0:T(8,128)S(1)} copy(f32[8,32,16,128]{3,2,1,0:T(8,128)} %param.7) | data formatting | bytes 4194304 | tf_op args[0]
  4.2 4.5 %collective-permute-start.1 = (f32[8,6,32,128]{3,2,1,0:T(8,128)}, f32[8,6,32,128]{3,2,1,0:T(8,128)}, u32[]{:S(2)}, u32[]{:S(2)}) collective-permute-start(f32[8,6,32,128]{3,2,1,0:T(8,128)} %get-tuple-element.27), channel_id=1, source_target_pairs={{0,7},{1,0},{2,1},{3,2},{4,3},{5,4},{6,5},{7,6},{8,15},{9,8},{10,9... | collective-permute-start | bytes 2359304 | tf_op jit(solution)/shard_map/ppermute | solution.py:20
  9.4 3.5 %collective-permute-start.13 = (f32[6,32,32]{2,1,0:T(8,128)}, f32[6,32,32]{2,1,0:T(8,128)}, u32[]{:S(2)}, u32[]{:S(2)}) collective-permute-start(f32[6,32,32]{2,1,0:T(8,128)} %get-tuple-element.49), channel_id=1, source_target_pairs={{0,7},{1,0},{2,1},{3,2},{4,3},{5,4},{6,5},{7,6},{8,15},{9,8},{10,9... | collective-permute-start | bytes 73736 | tf_op jit(solution)/shard_map/ppermute | solution.py:20
  28.0 1.5 collective-permute-start.6
  30.1 1.5 collective-permute-start.20
  35.3 9.0 %collective-permute-done.31 = f32[1,8,32,128]{3,2,1,0:T(8,128)S(1)} collective-permute-done((f32[1,8,32,128]{3,2,1,0:T(8,128)}, f32[1,8,32,128]{3,2,1,0:T(8,128)S(1)}, u32[]{:S(2)}, u32[]{:S(2)}) %collective-permute-start.31) | collective-permute-done | bytes 131104 | tf_op jit(solution)/shard_map/ppermute | solution.py:15
  47.1 2.2 %collective-permute-done.14 = f32[1,7,32,128]{3,2,1,0:T(8,128)S(1)} collective-permute-done((f32[1,7,32,128]{3,2,1,0:T(8,128)}, f32[1,7,32,128]{3,2,1,0:T(8,128)S(1)}, u32[]{:S(2)}, u32[]{:S(2)}) %collective-permute-start.14) | collective-permute-done | bytes 114720 | tf_op jit(solution)/shard_map/ppermute | solution.py:15
  50.0 1.5 collective-permute-start.27
  55.9 2.9 %collective-permute-done.32 = f32[1,4,32,128]{3,2,1,0:T(8,128)S(1)} collective-permute-done((f32[1,4,32,128]{3,2,1,0:T(8,128)S(1)}, f32[1,4,32,128]{3,2,1,0:T(8,128)S(1)}, u32[]{:S(2)}, u32[]{:S(2)}) %collective-permute-start.32) | collective-permute-done | bytes 65568 | tf_op jit(solution)/shard_map/ppermute | solution.py:15
  59.4 1.6 collective-permute-start.15
  62.8 2.4 %collective-permute-done.16 = f32[2,8,32,128]{3,2,1,0:T(8,128)S(1)} collective-permute-done((f32[2,8,32,128]{3,2,1,0:T(8,128)S(1)}, f32[2,8,32,128]{3,2,1,0:T(8,128)S(1)}, u32[]{:S(2)}, u32[]{:S(2)}) %collective-permute-start.16) | collective-permute-done | bytes 262176 | tf_op jit(solution)/shard_map/ppermute | solution.py:15
  66.6 2.9 %collective-permute-done.33 = f32[1,4,32,128]{3,2,1,0:T(8,128)S(1)} collective-permute-done((f32[1,4,32,128]{3,2,1,0:T(8,128)S(1)}, f32[1,4,32,128]{3,2,1,0:T(8,128)S(1)}, u32[]{:S(2)}, u32[]{:S(2)}) %collective-permute-start.33) | collective-permute-done | bytes 65568 | tf_op jit(solution)/shard_map/ppermute | solution.py:15
  71.0 2.7 %collective-permute-done.28 = f32[1,4,32,128]{3,2,1,0:T(8,128)S(1)} collective-permute-done((f32[1,4,32,128]{3,2,1,0:T(8,128)S(1)}, f32[1,4,32,128]{3,2,1,0:T(8,128)S(1)}, u32[]{:S(2)}, u32[]{:S(2)}) %collective-permute-start.28) | collective-permute-done | bytes 65568 | tf_op jit(solution)/shard_map/ppermute | solution.py:15
  77.0 1.5 collective-permute-start.17
  82.6 1.6 collective-permute-start.29
  92.7 2.7 %collective-permute-done.2 = f32[3,8,32,128]{3,2,1,0:T(8,128)S(1)} collective-permute-done((f32[3,8,32,128]{3,2,1,0:T(8,128)S(1)}, f32[3,8,32,128]{3,2,1,0:T(8,128)S(1)}, u32[]{:S(2)}, u32[]{:S(2)}) %collective-permute-start.2) | collective-permute-done | bytes 393248 | tf_op jit(solution)/shard_map/ppermute | solution.py:15
  99.0 1.6 collective-permute-start.23
  100.6 1.9 %collective-permute-done.7 = f32[3,4,32,128]{3,2,1,0:T(8,128)S(1)} collective-permute-done((f32[3,4,32,128]{3,2,1,0:T(8,128)S(1)}, f32[3,4,32,128]{3,2,1,0:T(8,128)S(1)}, u32[]{:S(2)}, u32[]{:S(2)}) %collective-permute-start.7) | collective-permute-done | bytes 196640 | tf_op jit(solution)/shard_map/ppermute | solution.py:15
  104.8 4.3 %collective-permute-done.23 = f32[2,8,32,128]{3,2,1,0:T(8,128)S(1)} collective-permute-done((f32[2,8,32,128]{3,2,1,0:T(8,128)S(1)}, f32[2,8,32,128]{3,2,1,0:T(8,128)S(1)}, u32[]{:S(2)}, u32[]{:S(2)}) %collective-permute-start.23) | collective-permute-done | bytes 262176 | tf_op jit(solution)/shard_map/ppermute | solution.py:15
  110.0 4.7 %collective-permute-start.25 = (f32[2,5,32,128]{3,2,1,0:T(8,128)S(1)}, f32[2,5,32,128]{3,2,1,0:T(8,128)S(1)}, u32[]{:S(2)}, u32[]{:S(2)}) collective-permute-start(f32[2,5,32,128]{3,2,1,0:T(8,128)S(1)} %pad_maximum_fusion.10), channel_id=1, source_target_pairs={{0,7},{1,0},{2,1},{3,2},{4,3},{5,4},{6,5},{7,6},{8,15},{9,8},{10,9... | collective-permute-start | bytes 491528 | tf_op jit(solution)/shard_map/ppermute | solution.py:20
  114.7 1.6 collective-permute-start.9
  117.7 3.7 %pad_maximum_fusion.field_hbm = f32[8,28,32,128]{3,2,1,0:T(8,128)} fusion(f32[8,6,32,128]{3,2,1,0:T(8,128)} %collective-permute-done.1, f32[8,16,32,128]{3,2,1,0:T(8,128)S(1)} %bitcast.71, f32[8,6,32,128]{3,2,1,0:T(8,128)} %collective-permute-done), kind=kLoop, calls=%fused_computation | loop fusion | flops 1835008 | bytes 7340032 | tf_op jit(solution)/shard_map/concatenate | solution.py:167
  121.4 5.3 %collective-permute-done.9 = f32[3,8,32,128]{3,2,1,0:T(8,128)S(1)} collective-permute-done((f32[3,8,32,128]{3,2,1,0:T(8,128)S(1)}, f32[3,8,32,128]{3,2,1,0:T(8,128)S(1)}, u32[]{:S(2)}, u32[]{:S(2)}) %collective-permute-start.9) | collective-permute-done | bytes 393248 | tf_op jit(solution)/shard_map/ppermute | solution.py:15
  127.0 1.8 collective-permute-start.10
  128.9 1.8 collective-permute-start.11
  130.9 7.7 %collective-permute-done.10 = f32[3,10,32,128]{3,2,1,0:T(8,128)S(1)} collective-permute-done((f32[3,10,32,128]{3,2,1,0:T(8,128)S(1)}, f32[3,10,32,128]{3,2,1,0:T(8,128)S(1)}, u32[]{:S(2)}, u32[]{:S(2)}) %collective-permute-start.10) | collective-permute-done | bytes 491552 | tf_op jit(solution)/shard_map/ppermute | solution.py:20
  138.6 2.6 %collective-permute-done.11 = f32[3,11,32,128]{3,2,1,0:T(8,128)S(1)} collective-permute-done((f32[3,11,32,128]{3,2,1,0:T(8,128)S(1)}, f32[3,11,32,128]{3,2,1,0:T(8,128)S(1)}, u32[]{:S(2)}, u32[]{:S(2)}) %collective-permute-start.11) | collective-permute-done | bytes 540704 | tf_op jit(solution)/shard_map/ppermute | solution.py:20
  142.0 24.7 %steps_0.1 = (f32[8,28,32,128]{3,2,1,0:T(8,128)}, f32[8,16,128]{2,1,0:T(8,128)S(1)}) custom-call(s32[6]{0:T(128)S(1)} %copy-done.1, s32[8]{0:T(128)S(1)} %copy-done.2, s32[8]{0:T(128)S(1)} %copy-done.3, s32[8]{0:T(128)S(1)} %copy-done.4, s32[1]{0:T(128)} %bitcast.start_ref, f32[8,28,32,128]{3,2,1,0:T(8,128)} %pad_maximum_fusion.field_hbm, ...), custom_call_target="tpu_custom_call" | custom-call | flops 550502400 | bytes 7340032 | tf_op jit(solution)/shard_map/steps_0/pallas_call | solution.py:139
  166.8 13.3 %steps_3.1 = (f32[8,28,32,128]{3,2,1,0:T(8,128)S(1)}, f32[8,16,128]{2,1,0:T(8,128)S(1)}) custom-call(s32[6]{0:T(128)S(1)} %copy-done.1, s32[8]{0:T(128)S(1)} %copy-done.2, s32[8]{0:T(128)S(1)} %copy-done.3, s32[8]{0:T(128)S(1)} %copy-done.4, s32[1]{0:T(128)} %bitcast.start_ref, f32[8,28,32,128]{3,2,1,0:T(8,128)} %get-tuple-element.8.field_hbm, ...), custom_call_target="tpu_custom_call" | custom-call | flops 367001600 | bytes 7340032 | tf_op jit(solution)/shard_map/steps_3/pallas_call | solution.py:139
  180.1 1.8 copy-done
  181.9 7.7 %steps_5.1 = (f32[8,28,32,128]{3,2,1,0:T(8,128)S(1)}, f32[8,16,128]{2,1,0:T(8,128)}) custom-call(s32[6]{0:T(128)S(1)} %copy-done.1, s32[8]{0:T(128)S(1)} %copy-done.2, s32[8]{0:T(128)S(1)} %copy-done.3, s32[8]{0:T(128)S(1)} %copy-done.4, s32[1]{0:T(128)} %bitcast.start_ref, f32[8,28,32,128]{3,2,1,0:T(8,128)} %copy-done, ...), custom_call_target="tpu_custom_call" | custom-call | flops 183500800 | bytes 7340032 | tf_op jit(solution)/shard_map/steps_5/pallas_call | solution.py:139
  189.9 2.5 %copy.56 = f32[8,32,16,128]{3,2,1,0:T(8,128)} copy(f32[8,32,16,128]{3,1,2,0:T(8,128)S(1)} %slice_bitcast_fusion) | data formatting | bytes 4194304
  (191 shorter events, 58.2 us)
Async XLA Ops:
  4.2 112.6 %collective-permute-start.1 = (f32[8,6,32,128]{3,2,1,0:T(8,128)}, f32[8,6,32,128]{3,2,1,0:T(8,128)}, u32[]{:S(2)}, u32[]{:S(2)}) collective-permute-start(f32[8,6,32,128]{3,2,1,0:T(8,128)} %get-tuple-element.27), channel_id=1, source_target_pairs={{0,7},{1,0},{2,1},{3,2},{4,3},{5,4},{6,5},{7,6},{8,15},{9,8},{10,9... | collective-permute-start | bytes 2359304 | tf_op jit(solution)/shard_map/ppermute | solution.py:20
  8.7 109.0 %collective-permute-start = (f32[8,6,32,128]{3,2,1,0:T(8,128)}, f32[8,6,32,128]{3,2,1,0:T(8,128)}, u32[]{:S(2)}, u32[]{:S(2)}) collective-permute-start(f32[8,6,32,128]{3,2,1,0:T(8,128)} %get-tuple-element.26), channel_id=1, source_target_pairs={{0,1},{1,2},{2,3},{3,4},{4,5},{5,6},{6,7},{7,0},{8,9},{9,10},{10,1... | collective-permute-start | bytes 2359304 | tf_op jit(solution)/shard_map/ppermute | solution.py:20
  9.4 18.6 %collective-permute-start.13 = (f32[6,32,32]{2,1,0:T(8,128)}, f32[6,32,32]{2,1,0:T(8,128)}, u32[]{:S(2)}, u32[]{:S(2)}) collective-permute-start(f32[6,32,32]{2,1,0:T(8,128)} %get-tuple-element.49), channel_id=1, source_target_pairs={{0,7},{1,0},{2,1},{3,2},{4,3},{5,4},{6,5},{7,6},{8,15},{9,8},{10,9... | collective-permute-start | bytes 73736 | tf_op jit(solution)/shard_map/ppermute | solution.py:20
  12.9 17.1 %collective-permute-start.12 = (f32[6,32,32]{2,1,0:T(8,128)}, f32[6,32,32]{2,1,0:T(8,128)}, u32[]{:S(2)}, u32[]{:S(2)}) collective-permute-start(f32[6,32,32]{2,1,0:T(8,128)} %get-tuple-element.48), channel_id=1, source_target_pairs={{0,1},{1,2},{2,3},{3,4},{4,5},{5,6},{6,7},{7,0},{8,9},{9,10},{10,1... | collective-permute-start | bytes 73736 | tf_op jit(solution)/shard_map/ppermute | solution.py:20
  15.4 18.4 %collective-permute-start.26 = (f32[1,8,32,128]{3,2,1,0:T(8,128)}, f32[1,8,32,128]{3,2,1,0:T(8,128)}, u32[]{:S(2)}, u32[]{:S(2)}) collective-permute-start(f32[1,8,32,128]{3,2,1,0:T(8,128)} %bitcast.69), channel_id=1, source_target_pairs={{0,8},{8,0},{16,24},{24,16},{1,9},{9,1},{17,25},{25,17},{2,10},{10... | collective-permute-start | bytes 393224 | tf_op jit(solution)/shard_map/ppermute | solution.py:15
  28.0 62.8 %collective-permute-start.6 = (f32[3,8,32,128]{3,2,1,0:T(8,128)}, f32[3,8,32,128]{3,2,1,0:T(8,128)}, u32[]{:S(2)}, u32[]{:S(2)}) collective-permute-start(f32[3,8,32,128]{3,2,1,0:T(8,128)} %bitcast.81), channel_id=1, source_target_pairs={{0,16},{8,24},{16,0},{24,8},{1,17},{9,25},{17,1},{25,9},{2,18},{10... | collective-permute-start | bytes 1179656 | tf_op jit(solution)/shard_map/ppermute | solution.py:15
  30.1 29.3 %collective-permute-start.20 = (f32[2,8,32,128]{3,2,1,0:T(8,128)}, f32[2,8,32,128]{3,2,1,0:T(8,128)}, u32[]{:S(2)}, u32[]{:S(2)}) collective-permute-start(f32[2,8,32,128]{3,2,1,0:T(8,128)} %bitcast.66), channel_id=1, source_target_pairs={{0,16},{8,24},{16,0},{24,8},{1,17},{9,25},{17,1},{25,9},{2,18},{10... | collective-permute-start | bytes 786440 | tf_op jit(solution)/shard_map/ppermute | solution.py:15
  33.8 10.5 %collective-permute-start.31 = (f32[1,8,32,128]{3,2,1,0:T(8,128)}, f32[1,8,32,128]{3,2,1,0:T(8,128)S(1)}, u32[]{:S(2)}, u32[]{:S(2)}) collective-permute-start(f32[1,8,32,128]{3,2,1,0:T(8,128)} %bitcast.68), channel_id=1, source_target_pairs={{0,16},{8,24},{16,0},{24,8},{1,17},{9,25},{17,1},{25,9},{2,18},{10... | collective-permute-start | bytes 393224 | tf_op jit(solution)/shard_map/ppermute | solution.py:15
  44.3 5.0 %collective-permute-start.14 = (f32[1,7,32,128]{3,2,1,0:T(8,128)}, f32[1,7,32,128]{3,2,1,0:T(8,128)S(1)}, u32[]{:S(2)}, u32[]{:S(2)}) collective-permute-start(f32[1,7,32,128]{3,2,1,0:T(8,128)} %reshape.387), channel_id=1, source_target_pairs={{0,8},{8,0},{16,24},{24,16},{1,9},{9,1},{17,25},{25,17},{2,10},{10... | collective-permute-start | bytes 344072 | tf_op jit(solution)/shard_map/ppermute | solution.py:15
  50.0 4.6 %collective-permute-start.27 = (f32[1,4,32,128]{3,2,1,0:T(8,128)}, f32[1,4,32,128]{3,2,1,0:T(8,128)}, u32[]{:S(2)}, u32[]{:S(2)}) collective-permute-start(f32[1,4,32,128]{3,2,1,0:T(8,128)} %constant_dynamic-slice_fusion.3), channel_id=1, source_target_pairs={{0,16},{8,24},{16,0},{24,8},{1,17},{9,25},{17,1},{25,9},{2,18},{10... | collective-permute-start | bytes 196616 | tf_op jit(solution)/shard_map/ppermute | solution.py:15
  54.6 4.3 %collective-permute-start.32 = (f32[1,4,32,128]{3,2,1,0:T(8,128)S(1)}, f32[1,4,32,128]{3,2,1,0:T(8,128)S(1)}, u32[]{:S(2)}, u32[]{:S(2)}) collective-permute-start(f32[1,4,32,128]{3,2,1,0:T(8,128)S(1)} %copy-done.28), channel_id=1, source_target_pairs={{0,8},{8,0},{16,24},{24,16},{1,9},{9,1},{17,25},{25,17},{2,10},{10... | collective-permute-start | bytes 196616 | tf_op jit(solution)/shard_map/ppermute | solution.py:15
  58.8 6.4 %collective-permute-start.16 = (f32[2,8,32,128]{3,2,1,0:T(8,128)S(1)}, f32[2,8,32,128]{3,2,1,0:T(8,128)S(1)}, u32[]{:S(2)}, u32[]{:S(2)}) collective-permute-start(f32[2,8,32,128]{3,2,1,0:T(8,128)S(1)} %bitcast.82), channel_id=1, source_target_pairs={{0,8},{8,0},{16,24},{24,16},{1,9},{9,1},{17,25},{25,17},{2,10},{10... | collective-permute-start | bytes 786440 | tf_op jit(solution)/shard_map/ppermute | solution.py:15
  59.4 16.9 %collective-permute-start.15 = (f32[2,7,32,128]{3,2,1,0:T(8,128)S(1)}, f32[2,7,32,128]{3,2,1,0:T(8,128)S(1)}, u32[]{:S(2)}, u32[]{:S(2)}) collective-permute-start(f32[2,7,32,128]{3,2,1,0:T(8,128)S(1)} %maximum_select_fusion.12), channel_id=1, source_target_pairs={{0,16},{8,24},{16,0},{24,8},{1,17},{9,25},{17,1},{25,9},{2,18},{10... | collective-permute-start | bytes 688136 | tf_op jit(solution)/shard_map/ppermute | solution.py:15
  73.7 8.8 %collective-permute-start.21 = (f32[2,4,32,128]{3,2,1,0:T(8,128)}, f32[2,4,32,128]{3,2,1,0:T(8,128)}, u32[]{:S(2)}, u32[]{:S(2)}) collective-permute-start(f32[2,4,32,128]{3,2,1,0:T(8,128)} %constant_dynamic-slice_fusion.6), channel_id=1, source_target_pairs={{0,8},{8,0},{16,24},{24,16},{1,9},{9,1},{17,25},{25,17},{2,10},{10... | collective-permute-start | bytes 393224 | tf_op jit(solution)/shard_map/ppermute | solution.py:15
  77.0 8.2 %collective-permute-start.17 = (f32[2,4,32,128]{3,2,1,0:T(8,128)}, f32[2,4,32,128]{3,2,1,0:T(8,128)}, u32[]{:S(2)}, u32[]{:S(2)}) collective-permute-start(f32[2,4,32,128]{3,2,1,0:T(8,128)} %constant_dynamic-slice_fusion.9), channel_id=1, source_target_pairs={{0,16},{8,24},{16,0},{24,8},{1,17},{9,25},{17,1},{25,9},{2,18},{10... | collective-permute-start | bytes 393224 | tf_op jit(solution)/shard_map/ppermute | solution.py:15
  82.6 5.0 %collective-permute-start.29 = (f32[1,8,32,128]{3,2,1,0:T(8,128)S(1)}, f32[1,8,32,128]{3,2,1,0:T(8,128)S(1)}, u32[]{:S(2)}, u32[]{:S(2)}) collective-permute-start(f32[1,8,32,128]{3,2,1,0:T(8,128)S(1)} %copy-done.27), channel_id=1, source_target_pairs={{0,8},{8,0},{16,24},{24,16},{1,9},{9,1},{17,25},{25,17},{2,10},{10... | collective-permute-start | bytes 393224 | tf_op jit(solution)/shard_map/ppermute | solution.py:15
  85.1 5.0 %collective-permute-start.34 = (f32[1,8,32,128]{3,2,1,0:T(8,128)S(1)}, f32[1,8,32,128]{3,2,1,0:T(8,128)S(1)}, u32[]{:S(2)}, u32[]{:S(2)}) collective-permute-start(f32[1,8,32,128]{3,2,1,0:T(8,128)S(1)} %copy-done.26), channel_id=1, source_target_pairs={{0,16},{8,24},{16,0},{24,8},{1,17},{9,25},{17,1},{25,9},{2,18},{10... | collective-permute-start | bytes 393224 | tf_op jit(solution)/shard_map/ppermute | solution.py:15
  87.6 7.8 %collective-permute-start.2 = (f32[3,8,32,128]{3,2,1,0:T(8,128)S(1)}, f32[3,8,32,128]{3,2,1,0:T(8,128)S(1)}, u32[]{:S(2)}, u32[]{:S(2)}) collective-permute-start(f32[3,8,32,128]{3,2,1,0:T(8,128)S(1)} %bitcast.80), channel_id=1, source_target_pairs={{0,8},{8,0},{16,24},{24,16},{1,9},{9,1},{17,25},{25,17},{2,10},{10... | collective-permute-start | bytes 1179656 | tf_op jit(solution)/shard_map/ppermute | solution.py:15
  90.2 8.2 %collective-permute-start.22 = (f32[2,4,32,128]{3,2,1,0:T(8,128)S(1)}, f32[2,4,32,128]{3,2,1,0:T(8,128)S(1)}, u32[]{:S(2)}, u32[]{:S(2)}) collective-permute-start(f32[2,4,32,128]{3,2,1,0:T(8,128)S(1)} %dynamic-slice_select_fusion.2), channel_id=1, source_target_pairs={{0,8},{8,0},{16,24},{24,16},{1,9},{9,1},{17,25},{25,17},{2,10},{10... | collective-permute-start | bytes 393224 | tf_op jit(solution)/shard_map/ppermute | solution.py:15
  90.8 8.2 %collective-permute-start.18 = (f32[2,4,32,128]{3,2,1,0:T(8,128)S(1)}, f32[2,4,32,128]{3,2,1,0:T(8,128)S(1)}, u32[]{:S(2)}, u32[]{:S(2)}) collective-permute-start(f32[2,4,32,128]{3,2,1,0:T(8,128)S(1)} %dynamic-slice_select_fusion.3), channel_id=1, source_target_pairs={{0,16},{8,24},{16,0},{24,8},{1,17},{9,25},{17,1},{25,9},{2,18},{10... | collective-permute-start | bytes 393224 | tf_op jit(solution)/shard_map/ppermute | solution.py:15
  96.8 5.7 %collective-permute-start.7 = (f32[3,4,32,128]{3,2,1,0:T(8,128)S(1)}, f32[3,4,32,128]{3,2,1,0:T(8,128)S(1)}, u32[]{:S(2)}, u32[]{:S(2)}) collective-permute-start(f32[3,4,32,128]{3,2,1,0:T(8,128)S(1)} %constant_dynamic-slice_fusion.12), channel_id=1, source_target_pairs={{0,8},{8,0},{16,24},{24,16},{1,9},{9,1},{17,25},{25,17},{2,10},{10... | collective-permute-start | bytes 589832 | tf_op jit(solution)/shard_map/ppermute | solution.py:15
  98.4 5.7 %collective-permute-start.3 = (f32[3,4,32,128]{3,2,1,0:T(8,128)S(1)}, f32[3,4,32,128]{3,2,1,0:T(8,128)S(1)}, u32[]{:S(2)}, u32[]{:S(2)}) collective-permute-start(f32[3,4,32,128]{3,2,1,0:T(8,128)S(1)} %constant_dynamic-slice_fusion.15), channel_id=1, source_target_pairs={{0,16},{8,24},{16,0},{24,8},{1,17},{9,25},{17,1},{25,9},{2,18},{10... | collective-permute-start | bytes 589832 | tf_op jit(solution)/shard_map/ppermute | solution.py:15
  99.0 10.1 %collective-permute-start.23 = (f32[2,8,32,128]{3,2,1,0:T(8,128)S(1)}, f32[2,8,32,128]{3,2,1,0:T(8,128)S(1)}, u32[]{:S(2)}, u32[]{:S(2)}) collective-permute-start(f32[2,8,32,128]{3,2,1,0:T(8,128)S(1)} %maximum_select_fusion.9), channel_id=1, source_target_pairs={{0,16},{8,24},{16,0},{24,8},{1,17},{9,25},{17,1},{25,9},{2,18},{10... | collective-permute-start | bytes 786440 | tf_op jit(solution)/shard_map/ppermute | solution.py:15
  102.5 7.4 %collective-permute-start.19 = (f32[2,8,32,128]{3,2,1,0:T(8,128)S(1)}, f32[2,8,32,128]{3,2,1,0:T(8,128)S(1)}, u32[]{:S(2)}, u32[]{:S(2)}) collective-permute-start(f32[2,8,32,128]{3,2,1,0:T(8,128)S(1)} %maximum_select_fusion.8), channel_id=1, source_target_pairs={{0,8},{8,0},{16,24},{24,16},{1,9},{9,1},{17,25},{25,17},{2,10},{10... | collective-permute-start | bytes 786440 | tf_op jit(solution)/shard_map/ppermute | solution.py:15
  104.1 10.6 %collective-permute-start.8 = (f32[3,4,32,128]{3,2,1,0:T(8,128)S(1)}, f32[3,4,32,128]{3,2,1,0:T(8,128)S(1)}, u32[]{:S(2)}, u32[]{:S(2)}) collective-permute-start(f32[3,4,32,128]{3,2,1,0:T(8,128)S(1)} %dynamic-slice_select_fusion), channel_id=1, source_target_pairs={{0,8},{8,0},{16,24},{24,16},{1,9},{9,1},{17,25},{25,17},{2,10},{10... | collective-permute-start | bytes 589832 | tf_op jit(solution)/shard_map/ppermute | solution.py:15
  109.1 7.2 %collective-permute-start.4 = (f32[3,4,32,128]{3,2,1,0:T(8,128)S(1)}, f32[3,4,32,128]{3,2,1,0:T(8,128)S(1)}, u32[]{:S(2)}, u32[]{:S(2)}) collective-permute-start(f32[3,4,32,128]{3,2,1,0:T(8,128)S(1)} %dynamic-slice_select_fusion.1), channel_id=1, source_target_pairs={{0,16},{8,24},{16,0},{24,8},{1,17},{9,25},{17,1},{25,9},{2,18},{10... | collective-permute-start | bytes 589832 | tf_op jit(solution)/shard_map/ppermute | solution.py:15
  110.0 20.7 %collective-permute-start.25 = (f32[2,5,32,128]{3,2,1,0:T(8,128)S(1)}, f32[2,5,32,128]{3,2,1,0:T(8,128)S(1)}, u32[]{:S(2)}, u32[]{:S(2)}) collective-permute-start(f32[2,5,32,128]{3,2,1,0:T(8,128)S(1)} %pad_maximum_fusion.10), channel_id=1, source_target_pairs={{0,7},{1,0},{2,1},{3,2},{4,3},{5,4},{6,5},{7,6},{8,15},{9,8},{10,9... | collective-permute-start | bytes 491528 | tf_op jit(solution)/shard_map/ppermute | solution.py:20
  114.7 12.0 %collective-permute-start.9 = (f32[3,8,32,128]{3,2,1,0:T(8,128)S(1)}, f32[3,8,32,128]{3,2,1,0:T(8,128)S(1)}, u32[]{:S(2)}, u32[]{:S(2)}) collective-permute-start(f32[3,8,32,128]{3,2,1,0:T(8,128)S(1)} %maximum_select_fusion.7), channel_id=1, source_target_pairs={{0,16},{8,24},{16,0},{24,8},{1,17},{9,25},{17,1},{25,9},{2,18},{10... | collective-permute-start | bytes 1179656 | tf_op jit(solution)/shard_map/ppermute | solution.py:15
  116.3 14.4 %collective-permute-start.24 = (f32[2,4,32,128]{3,2,1,0:T(8,128)S(1)}, f32[2,4,32,128]{3,2,1,0:T(8,128)S(1)}, u32[]{:S(2)}, u32[]{:S(2)}) collective-permute-start(f32[2,4,32,128]{3,2,1,0:T(8,128)S(1)} %pad_maximum_fusion.11), channel_id=1, source_target_pairs={{0,1},{1,2},{2,3},{3,4},{4,5},{5,6},{6,7},{7,0},{8,9},{9,10},{10,1... | collective-permute-start | bytes 393224 | tf_op jit(solution)/shard_map/ppermute | solution.py:20
  116.8 10.1 %collective-permute-start.5 = (f32[3,8,32,128]{3,2,1,0:T(8,128)S(1)}, f32[3,8,32,128]{3,2,1,0:T(8,128)S(1)}, u32[]{:S(2)}, u32[]{:S(2)}) collective-permute-start(f32[3,8,32,128]{3,2,1,0:T(8,128)S(1)} %maximum_select_fusion.6), channel_id=1, source_target_pairs={{0,8},{8,0},{16,24},{24,16},{1,9},{9,1},{17,25},{25,17},{2,10},{10... | collective-permute-start | bytes 1179656 | tf_op jit(solution)/shard_map/ppermute | solution.py:15
  127.0 11.5 %collective-permute-start.10 = (f32[3,10,32,128]{3,2,1,0:T(8,128)S(1)}, f32[3,10,32,128]{3,2,1,0:T(8,128)S(1)}, u32[]{:S(2)}, u32[]{:S(2)}) collective-permute-start(f32[3,10,32,128]{3,2,1,0:T(8,128)S(1)} %pad_maximum_fusion.7), channel_id=1, source_target_pairs={{0,1},{1,2},{2,3},{3,4},{4,5},{5,6},{6,7},{7,0},{8,9},{9,10},{10,1... | collective-permute-start | bytes 1474568 | tf_op jit(solution)/shard_map/ppermute | solution.py:20
  128.9 12.3 %collective-permute-start.11 = (f32[3,11,32,128]{3,2,1,0:T(8,128)S(1)}, f32[3,11,32,128]{3,2,1,0:T(8,128)S(1)}, u32[]{:S(2)}, u32[]{:S(2)}) collective-permute-start(f32[3,11,32,128]{3,2,1,0:T(8,128)S(1)} %pad_maximum_fusion.6), channel_id=1, source_target_pairs={{0,7},{1,0},{2,1},{3,2},{4,3},{5,4},{6,5},{7,6},{8,15},{9,8},{10,9... | collective-permute-start | bytes 1622024 | tf_op jit(solution)/shard_map/ppermute | solution.py:20
  (34 other events, 157.5 us)

commit v2 on v1

v2 whole, which is shorter than its diff:
```python
import functools

import jax
import jax.numpy as jnp
from jax import lax
from jax.experimental import pallas as pl
from jax.experimental.pallas import tpu as pltpu
from jax.sharding import PartitionSpec as P

CHUNKS = ((0, 1, 2), (3, 4, 5))
PARTS = 4
SMEM = pl.BlockSpec(memory_space=pltpu.SMEM)
VMEM = pl.BlockSpec(memory_space=pltpu.VMEM)
LIMIT = pltpu.CompilerParams(vmem_limit_bytes=48 << 20)


def cost(nbytes):
    return pl.CostEstimate(flops=int(nbytes), bytes_accessed=int(nbytes), transcendentals=0)


def flip(block, bit):
    count = lax.axis_size("rcp")
    return lax.ppermute(block, "rcp", [(i, i ^ (1 << bit)) for i in range(count)])


def along(block, distance):
    count = lax.axis_size("lon")
    return lax.ppermute(block, "lon", [(i, (i + distance) % count) for i in range(count)])


def owned_pieces(flux, owners):
    count = lax.axis_size("rcp")
    block = flux.shape[2] // PARTS
    me = lax.axis_index("rcp")
    if count != PARTS:
        mine = (owners == me)[None, :, None, None, None]
        full = lax.psum(jnp.where(mine, flux, 0.0), "rcp")
        cuts = [full[:, :, m * block:(m + 1) * block] for m in range(PARTS)]
        return [c[0] for c in cuts], [c[1] for c in cuts], jnp.arange(PARTS, dtype=jnp.int32)

    def piece(comp, mask):
        return lax.dynamic_slice_in_dim(flux[comp], (me ^ mask) * block, block, axis=1)

    same_x = ((owners & 1) == (me & 1))[:, None, None, None]
    same_y = ((owners >> 1) == (me >> 1))[:, None, None, None]
    from_x = flip(jnp.stack([piece(0, 3), piece(0, 1)]), 0)
    from_y = flip(jnp.stack([piece(1, 3), piece(1, 2)]), 1)
    v_x = flip(jnp.where(same_y, piece(1, 1), from_y[0]), 0)
    u_y = flip(jnp.where(same_x, piece(0, 2), from_x[0]), 1)
    u_own = jnp.where(same_y, jnp.where(same_x, piece(0, 0), from_x[1]), u_y)
    v_own = jnp.where(same_x, jnp.where(same_y, piece(1, 0), from_y[1]), v_x)
    u2, v1 = flip(u_own, 1), flip(v_own, 0)
    u1, v2 = flip(u_own, 0), flip(v_own, 1)
    u3, v3 = flip(u2, 0), flip(v1, 1)
    part = jnp.stack([me ^ m for m in range(PARTS)]).astype(jnp.int32)
    return [u_own, u1, u2, u3], [v_own, v1, v2, v3], part


def edge_entries(steps, width):
    west, east = [], []
    for k in range(steps):
        reach = steps - 1 - k
        west += [(0, k, c) for c in range(reach + 1)] + [(1, k, c) for c in range(reach)]
        east += [(comp, k, width - reach + c) for comp in (0, 1) for c in range(reach)]
    return west, east


def edges_kernel(entries, part_ref, *refs):
    block = refs[0].shape[1]
    pieces, outs = (refs[:PARTS], refs[PARTS:2 * PARTS]), refs[2 * PARTS:]
    for out, wanted in zip(outs, entries):
        for i, (comp, k, c) in enumerate(wanted):
            for m in range(PARTS):
                rows = pl.ds(pl.multiple_of(part_ref[m] * block, block), block)
                out[i, rows, :] = pieces[comp][m][k, :, c, :]


def pick_edges(part, u, v):
    steps, block, width, lat = u[0].shape
    entries = edge_entries(steps, width)
    outs = pl.pallas_call(
        functools.partial(edges_kernel, [e for e in entries if e]),
        out_shape=[jax.ShapeDtypeStruct((len(e), PARTS * block, lat), jnp.float32) for e in entries if e],
        in_specs=[SMEM] + [VMEM] * (2 * PARTS),
        out_specs=[VMEM] * sum(bool(e) for e in entries),
        compiler_params=LIMIT,
        cost_estimate=cost(8 * u[0].size * 4),
        name="edges",
    )(part, *u, *v)
    return outs if len(outs) == 2 else (outs[0], None)


def assemble_kernel(part_ref, *refs):
    pieces, outs = (refs[:PARTS], refs[PARTS:2 * PARTS]), refs[2 * PARTS:]
    steps, block = refs[0].shape[:2]
    for k in range(steps):
        for comp in (0, 1):
            for m in range(PARTS):
                rows = pl.ds(pl.multiple_of(part_ref[m] * block, block), block)
                outs[comp][k, :, rows, :] = jnp.swapaxes(pieces[comp][m][k], 0, 1)


def assemble(part, u, v):
    steps, block, width, lat = u[0].shape
    return pl.pallas_call(
        assemble_kernel,
        out_shape=[jax.ShapeDtypeStruct((steps, width, PARTS * block, lat), jnp.float32)] * 2,
        in_specs=[SMEM] + [VMEM] * (2 * PARTS),
        out_specs=[VMEM] * 2,
        compiler_params=LIMIT,
        cost_estimate=cost(16 * u[0].size * 4),
        name="assemble",
    )(part, *u, *v)


def mats_kernel(owner_ref, packed_ref, out_ref):
    steps, lev = out_ref.shape[0], out_ref.shape[2]
    groups, lanes = packed_ref.shape[1], packed_ref.shape[3]
    lane = lax.broadcasted_iota(jnp.int32, (lev, lanes), 1)
    for s in range(steps):
        for g in range(groups):
            packed = packed_ref[owner_ref[s], g]
            high = packed.astype(jnp.bfloat16).astype(jnp.float32)
            low = packed - high
            for k in range(lanes // lev):
                def at(x, place):
                    return pltpu.roll(x, (place - k) * lev % lanes, 1) if place != k else x
                row = jnp.where(lane < lev, at(high, 0), jnp.where(lane < 2 * lev, at(high, 1), at(low, 2)))
                out_ref[s, g * (lanes // lev) + k] = row[:, :3 * lev].astype(jnp.bfloat16)


def prepare_mats(mixing, owner, lat):
    width, lev, _ = mixing.shape
    pack = lat // lev
    packed = mixing.reshape(width // pack, pack, lev, lev).transpose(0, 2, 1, 3)
    packed = packed.reshape(width // pack, lev, lat)
    packed = jnp.concatenate([along(packed[-1:], 1), packed, along(packed[:1], -1)], axis=0)
    count = lax.axis_size("rcp")
    slots = packed[None]
    if count == PARTS:
        me = lax.axis_index("rcp")
        for bit in range(2):
            slots = jnp.concatenate([slots, flip(slots, bit)], axis=0)
        owner = owner ^ me.astype(owner.dtype)
    else:
        slots = lax.all_gather(slots, "rcp", axis=0, tiled=True)
    return pl.pallas_call(
        mats_kernel,
        out_shape=jax.ShapeDtypeStruct((owner.shape[0], width + 2 * pack, lev, 3 * lev), jnp.bfloat16),
        in_specs=[SMEM, VMEM],
        out_specs=VMEM,
        compiler_params=LIMIT,
        cost_estimate=cost(owner.shape[0] * width * lev * lat * 2),
        name="mats",
    )(owner, slots)


def steps_kernel(first_step, steps, edges, has_left, last_chunk, rlon_ref, rlat_ref, rel_ref, start_ref,
                 field_ref, west_ref, east_ref, foot_ref, u_ref, v_ref, mats_ref, right_ref, *rest):
    left_ref = None
    if has_left:
        left_ref, rest = rest[0], rest[1:]
    if last_chunk:
        out_ref, foot_out_ref, a_ref, b_ref, ue_ref, ve_ref = rest
    else:
        out_ref, wout_ref, eout_ref, foot_out_ref, a_ref, b_ref, ue_ref, ve_ref = rest
    halo = steps
    count, ext, lev, lat = a_ref.shape
    width = ext - 2 * halo
    reach = halo - 1
    nlon = width * lax.axis_size("lon")
    mat_pad = (mats_ref.shape[1] - width) // 2 - halo
    lane = lax.broadcasted_iota(jnp.int32, (lev, lat), 1)
    lane_row = lax.broadcasted_iota(jnp.int32, (1, lat), 1)
    first = lane == 0
    last = lane == lat - 1

    for r in range(count):
        a_ref[r, :halo] = west_ref[r]
        a_ref[r, halo + width:] = east_ref[r]
        if field_ref.shape[1] == lev and first_step == 0:
            a_ref[r, halo:halo + width] = jnp.swapaxes(field_ref[r], 0, 1)
        else:
            a_ref[r, halo:halo + width] = field_ref[r]
    for i, (comp, k, c) in enumerate(edges[0]):
        (ue_ref, ve_ref)[comp][k, reach + width + c] = right_ref[i]
    for i, (comp, k, c) in enumerate(edges[1]):
        (ue_ref, ve_ref)[comp][k, reach + c - width] = left_ref[i]
    for k in range(steps):
        ue_ref[k, reach:reach + width] = u_ref[k]
        ve_ref[k, reach:reach + width] = v_ref[k]
    foot_out_ref[...] = foot_ref[...]

    for k in range(steps):
        step = first_step + k
        src, dst = ((a_ref, b_ref), (b_ref, a_ref))[k % 2]
        for r in range(count):
            col = lax.rem(rlon_ref[r] - start_ref[0] + halo + nlon, nlon)

            @pl.when((rel_ref[r] == step) & (col < ext))
            def _():
                row = src[r, pl.ds(col, 1), 0:1, :]
                src[r, pl.ds(col, 1), 0:1, :] = row + jnp.where(
                    lane_row == rlat_ref[r], 1.0, 0.0
                )[None]

        def column(c, carry, src=src, dst=dst, k=k):
            j = c - 1
            uw = ue_ref[k, j]
            un = ue_ref[k, j + 1]
            v = ve_ref[k, j]
            vs = jnp.where(first, 0.0, v)
            vn = jnp.where(last, 0.0, pltpu.roll(v, lat - 1, 1))
            cw = jnp.maximum(uw, 0.0)
            ce = -jnp.minimum(un, 0.0)
            cs = jnp.maximum(vs, 0.0)
            cn = -jnp.minimum(vn, 0.0)
            c0 = 1.0 + (jnp.minimum(uw, 0.0) - jnp.maximum(un, 0.0)) + (
                jnp.minimum(vs, 0.0) - jnp.maximum(vn, 0.0)
            )
            his, los = [], []
            for r in range(count):
                q = src[r, c]
                p = c0 * q + cw * src[r, c - 1] + ce * src[r, c + 1]
                p = p + cs * pltpu.roll(q, 1, 1) + cn * pltpu.roll(q, lat - 1, 1)
                hi = p.astype(jnp.bfloat16)
                his.append(hi)
                los.append((p - hi.astype(jnp.float32)).astype(jnp.bfloat16))
            hi = jnp.concatenate(his, axis=1)
            lo = jnp.concatenate(los, axis=1)
            new = jnp.dot(
                mats_ref[step, c + mat_pad],
                jnp.concatenate([hi, lo, hi], axis=0),
                preferred_element_type=jnp.float32,
            )
            for r in range(count):
                dst[r, c] = new[:, r * lat:(r + 1) * lat]
            return carry

        lax.fori_loop(k + 1, ext - k - 1, column, 0, unroll=2)
        for r in range(count):
            foot_out_ref[r] = foot_out_ref[r] + dst[r, halo:halo + width, 0, :]

    final = (a_ref, b_ref)[steps % 2]
    for r in range(count):
        if last_chunk:
            out_ref[r] = jnp.swapaxes(final[r, halo:halo + width], 0, 1)
        else:
            out_ref[r] = final[r, halo:halo + width]
            wout_ref[r] = final[r, halo:halo + wout_ref.shape[1]]
            eout_ref[r] = final[r, halo + width - eout_ref.shape[1]:halo + width]


def run_steps(rows, next_halo, last_chunk, scalars, field, west, east, foot, u, v, mats, right, left):
    count, width, lat = foot.shape
    steps, lev = u.shape[0], u.shape[2]
    ext = width + 2 * steps
    tiles = jax.ShapeDtypeStruct
    if last_chunk:
        outs = [tiles((count, lev, width, lat), jnp.float32)]
    else:
        outs = [tiles((count, width, lev, lat), jnp.float32)]
        outs += [tiles((count, next_halo, lev, lat), jnp.float32)] * 2
    outs.append(tiles(foot.shape, jnp.float32))
    extra = [right] + ([left] if left is not None else [])
    return pl.pallas_call(
        functools.partial(
            steps_kernel, rows[0], steps, edge_entries(steps, width), left is not None, last_chunk
        ),
        out_shape=outs,
        in_specs=[SMEM] * 4 + [VMEM] * (7 + len(extra)),
        out_specs=[VMEM] * len(outs),
        scratch_shapes=[
            pltpu.VMEM((count, ext, lev, lat), jnp.float32),
            pltpu.VMEM((count, ext, lev, lat), jnp.float32),
            pltpu.VMEM((steps, width + 2 * steps - 1, lev, lat), jnp.float32),
            pltpu.VMEM((steps, width + 2 * steps - 2, lev, lat), jnp.float32),
        ],
        compiler_params=LIMIT,
        cost_estimate=pl.CostEstimate(
            flops=int(steps * count * width * lev * lev * lat * 6),
            bytes_accessed=int(8 * count * width * lev * lat), transcendentals=0,
        ),
        name="steps_%d" % rows[0],
    )(*scalars, field, west, east, foot, u, v, mats, *extra)


def local(adj_in, mass_flux, mixing, window_owner, receptor_lon, receptor_lat, release_step):
    count, lev, width, lat = adj_in.shape
    start = (lax.axis_index("lon") * width).astype(jnp.int32)[None]
    scalars = (receptor_lon, receptor_lat, release_step, start)
    field = adj_in
    halo = len(CHUNKS[0])
    east_edge = adj_in[:, :, width - halo:].transpose(0, 2, 1, 3)
    west_edge = adj_in[:, :, :halo].transpose(0, 2, 1, 3)
    mats = prepare_mats(mixing[0], window_owner, lat)
    foot = jnp.zeros((count, width, lat), jnp.float32)
    for n, rows in enumerate(CHUNKS):
        west, east = along(east_edge, 1), along(west_edge, -1)
        u, v, part = owned_pieces(mass_flux[0, :, rows[0]:rows[-1] + 1], window_owner[rows[0]:rows[-1] + 1])
        to_west, to_east = pick_edges(part, u, v)
        right = along(to_west, -1)
        left = along(to_east, 1) if to_east is not None else None
        u, v = assemble(part, u, v)
        last = n + 1 == len(CHUNKS)
        out = run_steps(rows, 0 if last else len(CHUNKS[n + 1]), last, scalars, field, west, east, foot,
                        u, v, mats, right, left)
        if last:
            return tuple(out)
        field, west_edge, east_edge, foot = out


def solution(mesh):
    return jax.shard_map(
        local,
        mesh=mesh,
        in_specs=(
            P("rcp", None, "lon", None),
            P("rcp", None, None, None, "lon", None),
            P("rcp", "lon", None, None),
            P(),
            P("rcp"),
            P("rcp"),
            P("rcp"),
        ),
        out_specs=(P("rcp", None, "lon", None), P("rcp", "lon", None)),
        check_vma=False,
    )
```

time: 195 us -> 120 us (0.62); the launches traced: 192 us -> 120 us
  waiting for transfers between devices: 51.1 us -> 26.9 us
  local copies, waits for them, and re-layouts: 30.1 us -> 9.2 us
  Pallas kernels: 45.8 us -> 31.1 us
  other arithmetic: 18.1 us -> 12.3 us
  starting transfers between devices: 44.5 us -> 39.4 us
    ppermute x26 -> x22, waiting for transfers between devices: 39.1 us -> 18 us  [flip(): return lax.ppermute(block, 'rcp', [(i, i ^ 1 << bit) for i in range(count)])]
    pallas_call x3 -> x7, Pallas kernels: 45.8 us -> 31.1 us  [the longest x2 27 us: run_steps(): pl.pallas_call(functools.partial(steps_kernel, rows[0], steps, edge_entri...]
    dynamic_slice x15 -> x0, local copies, waits for them, and re-layouts: 9.82 us -> none  [the longest x12 7.29 us: from_owner(): send = lax.dynamic_slice_in_dim(block, (1 - side) * half, half, axis=1)]
    concatenate x14 -> x2, other arithmetic: 6.61 us -> 0.04 us  [prepare_mats(): slots = jnp.concatenate([slots, flip(slots, bit)], axis=0)]
    unnamed x64 -> x30, local copies, waits for them, and re-layouts: 9.55 us -> 3.2 us
    ppermute x9 -> x10, starting transfers between devices: 16.8 us -> 11.8 us  [along(): lax.ppermute(block, 'lon', [(i, (i + distance) % count) for i in range(co...]
    ppermute x9 -> x10, waiting for transfers between devices: 12.1 us -> 8.9 us  [along(): lax.ppermute(block, 'lon', [(i, (i + distance) % count) for i in range(co...]
    concatenate x4 -> x0, local copies, waits for them, and re-layouts: 2.62 us -> none  [gather_slots(): jnp.concatenate([block, got], axis=0)]
  transfers between devices with their start and end apart: 35 -> 32, of which waited for: 17 -> 11; matrix products, arithmetic and copies ran while one was open for 19% -> 13% of each run, Pallas kernels for 0% -> 15%
where the time goes in v2:
time: 120 us
  starting transfers between devices  39.4 us (33%)
  Pallas kernels  31.1 us (26%)
  waiting for transfers between devices  26.9 us (22%)
  other arithmetic  12.3 us (10%)
  local copies, waits for them, and re-layouts  9.2 us (8%)
    ppermute x22, starting transfers between devices, flip(): return lax.ppermute(block, 'rcp', [(i, i ^ 1 << bit) for i in range(count)])  27.6 us
    pallas_call x2, Pallas kernels, run_steps(): pl.pallas_call(functools.partial(steps_kernel, rows[0], steps, edge_entri...  27 us
    ppermute x22, waiting for transfers between devices, flip(): return lax.ppermute(block, 'rcp', [(i, i ^ 1 << bit) for i in range(count)])  18 us
    ppermute x10, starting transfers between devices, along(): lax.ppermute(block, 'lon', [(i, (i + distance) % count) for i in range(co...  11.8 us
    ppermute x10, waiting for transfers between devices, along(): lax.ppermute(block, 'lon', [(i, (i + distance) % count) for i in range(co...  8.9 us
    select_n x2, other arithmetic, owned_pieces(): v_x = flip(jnp.where(same_y, piece(1, 1), from_y[0]), 0)  3.56 us
    select_n x2, other arithmetic, owned_pieces(): u_y = flip(jnp.where(same_x, piece(0, 2), from_x[0]), 1)  3.48 us
    slice x1, local copies, waits for them, and re-layouts, piece(): flux[comp]  3.28 us
  transfers between devices with their start and end apart: 32, of which 11 were waited for; matrix products, arithmetic and copies ran while one was open for 13% of the time, Pallas kernels for 15%

profile of v2, /device:TPU:0, one launch (start us, length us, event | category | flops | bytes accessed | tf_op | source)
XLA Modules:
  0.0 119.9 jit_solution(4130122991085598779)
XLA Ops:
  0.6 3.3 %fusion.12 = (f32[1,1,3,32,16,128]{5,4,3,2,1,0:T(8,128)S(1)}, f32[1,1,3,32,16,128]{5,4,3,2,1,0:T(8,128)S(1)}, f32[1,1,3,32,16,128]{5,4,3,2,1,0:T(8,128)}, f32[1,1,3,32,16,128]{5,4,3,2,1,0:T(8,128)}) fusion(f32[1,2,6,32,16,128]{5,4,3,2,1,0:T(8,128)} %param.8), kind=kLoop, calls=%fused_computation.44 | loop fusion | bytes 6291456 | tf_op jit(solution)/shard_map/slice | solution.py:42
  5.6 3.0 %collective-permute-start.7 = (f32[2,3,8,16,128]{4,3,2,1,0:T(8,128)}, f32[2,3,8,16,128]{4,3,2,1,0:T(8,128)}, u32[]{:S(2)}, u32[]{:S(2)}) collective-permute-start(f32[2,3,8,16,128]{4,3,2,1,0:T(8,128)} %pad_maximum_fusion.1), channel_id=1, source_target_pairs={{0,16},{8,24},{16,0},{24,8},{1,17},{9,25},{17,1},{25,9},{2,18},{10... | collective-permute-start | bytes 1179656 | tf_op jit(solution)/shard_map/ppermute | solution.py:23
  10.4 1.5 %collective-permute-start.2 = (f32[2,3,8,16,128]{4,3,2,1,0:T(8,128)}, f32[2,3,8,16,128]{4,3,2,1,0:T(8,128)}, u32[]{:S(2)}, u32[]{:S(2)}) collective-permute-start(f32[2,3,8,16,128]{4,3,2,1,0:T(8,128)} %pad_maximum_fusion), channel_id=1, source_target_pairs={{0,8},{8,0},{16,24},{24,16},{1,9},{9,1},{17,25},{25,17},{2,10},{10... | collective-permute-start | bytes 1179656 | tf_op jit(solution)/shard_map/ppermute | solution.py:23
  12.9 2.5 %collective-permute-start.13 = (f32[1,32,128]{2,1,0:T(8,128)S(1)}, f32[1,32,128]{2,1,0:T(8,128)S(1)}, u32[]{:S(2)}, u32[]{:S(2)}) collective-permute-start(f32[1,32,128]{2,1,0:T(8,128)S(1)} %slice.94), channel_id=1, source_target_pairs={{0,7},{1,0},{2,1},{3,2},{4,3},{5,4},{6,5},{7,6},{8,15},{9,8},{10,9... | collective-permute-start | bytes 49160 | tf_op jit(solution)/shard_map/ppermute | solution.py:28
  18.2 1.9 %fusion.6 = f32[3,8,16,128]{3,2,1,0:T(8,128)} fusion(f32[2,3,8,16,128]{4,3,2,1,0:T(8,128)} %collective-permute-done.7, f32[1,1,3,32,16,128]{5,4,3,2,1,0:T(8,128)} %copy-done.6, s32[]{:T(128)S(6)} %select_n.63, pred[3]{0:T(512)(128)(4,1)S(1)} %get-tuple-element.49), kind=kLoop, calls=%fused_computation.19 | loop fusion | flops 49152 | bytes 589831 | tf_op jit(solution)/shard_map/jit(_where)/select_n | solution.py:48
  20.1 2.1 %collective-permute-start.8 = (f32[3,8,16,128]{3,2,1,0:T(8,128)}, f32[3,8,16,128]{3,2,1,0:T(8,128)S(1)}, u32[]{:S(2)}, u32[]{:S(2)}) collective-permute-start(f32[3,8,16,128]{3,2,1,0:T(8,128)} %fusion.6), channel_id=1, source_target_pairs={{0,8},{8,0},{16,24},{24,16},{1,9},{9,1},{17,25},{25,17},{2,10},{10... | collective-permute-start | bytes 589832 | tf_op jit(solution)/shard_map/ppermute | solution.py:23
  22.2 1.8 %fusion.9 = f32[3,8,16,128]{3,2,1,0:T(8,128)} fusion(f32[2,3,8,16,128]{4,3,2,1,0:T(8,128)} %collective-permute-done.2, f32[1,1,3,32,16,128]{5,4,3,2,1,0:T(8,128)} %get-tuple-element.28, s32[]{:T(128)S(6)} %select_n.65, pred[3]{0:T(512)(128)(4,1)S(1)} %get-tuple-element.47), kind=kLoop, calls=%fused_computation.24 | loop fusion | flops 49152 | bytes 589831 | tf_op jit(solution)/shard_map/jit(_where)/select_n | solution.py:49
  24.0 2.0 %collective-permute-start.3 = (f32[3,8,16,128]{3,2,1,0:T(8,128)}, f32[3,8,16,128]{3,2,1,0:T(8,128)}, u32[]{:S(2)}, u32[]{:S(2)}) collective-permute-start(f32[3,8,16,128]{3,2,1,0:T(8,128)} %fusion.9), channel_id=1, source_target_pairs={{0,16},{8,24},{16,0},{24,8},{1,17},{9,25},{17,1},{25,9},{2,18},{10... | collective-permute-start | bytes 589832 | tf_op jit(solution)/shard_map/ppermute | solution.py:23
  27.8 2.1 %collective-permute-start.14 = (f32[1,6,32,128]{3,2,1,0:T(8,128)S(1)}, f32[1,6,32,128]{3,2,1,0:T(8,128)S(1)}, u32[]{:S(2)}, u32[]{:S(2)}) collective-permute-start(f32[1,6,32,128]{3,2,1,0:T(8,128)S(1)} %maximum_bitcast_fusion), channel_id=1, source_target_pairs={{0,8},{8,0},{16,24},{24,16},{1,9},{9,1},{17,25},{25,17},{2,10},{10... | collective-permute-start | bytes 294920 | tf_op jit(solution)/shard_map/ppermute | solution.py:23
  31.2 1.4 %fusion.8 = (f32[3,8,16,128]{3,2,1,0:T(8,128)S(1)}, f32[3,8,16,128]{3,2,1,0:T(8,128)S(1)}) fusion(f32[3,8,16,128]{3,2,1,0:T(8,128)S(1)} %collective-permute-done.8, f32[2,3,8,16,128]{4,3,2,1,0:T(8,128)} %collective-permute-done.7, f32[1,1,3,32,16,128]{5,4,3,2,1,0:T(8,128)} %copy-done.6, s32[]{:T(128)S(6)} %select_n.61, ...), kind=kLoop, calls=%fused_computation.22 | loop fusion | flops 196608 | bytes 1572874 | tf_op jit(solution)/shard_map/jit(_where)/select_n | solution.py:51
  33.9 1.7 %fusion = f32[3,8,16,128]{3,2,1,0:T(8,128)} fusion(f32[2,3,8,16,128]{4,3,2,1,0:T(8,128)} %collective-permute-done.25, f32[1,1,3,32,16,128]{5,4,3,2,1,0:T(8,128)S(1)} %get-tuple-element.26, s32[]{:T(128)S(6)} %select_n.63, pred[3]{0:T(512)(128)(4,1)S(1)} %get-tuple-element.46), kind=kLoop, calls=%fused_computation.9 | loop fusion | flops 49152 | bytes 589831 | tf_op jit(solution)/shard_map/jit(_where)/select_n | solution.py:48
  35.6 1.5 %collective-permute-start.4 = (f32[3,8,16,128]{3,2,1,0:T(8,128)S(1)}, f32[3,8,16,128]{3,2,1,0:T(8,128)S(1)}, u32[]{:S(2)}, u32[]{:S(2)}) collective-permute-start(f32[3,8,16,128]{3,2,1,0:T(8,128)S(1)} %get-tuple-element.45.refs_0_), channel_id=1, source_target_pairs={{0,8},{8,0},{16,24},{24,16},{1,9},{9,1},{17,25},{25,17},{2,10},{10... | collective-permute-start | bytes 589832 | tf_op jit(solution)/shard_map/ppermute | solution.py:23
  38.5 1.7 %collective-permute-start.6 = (f32[3,8,16,128]{3,2,1,0:T(8,128)S(1)}, f32[3,8,16,128]{3,2,1,0:T(8,128)S(1)}, u32[]{:S(2)}, u32[]{:S(2)}) collective-permute-start(f32[3,8,16,128]{3,2,1,0:T(8,128)S(1)} %collective-permute-done.5.refs_2_), channel_id=1, source_target_pairs={{0,8},{8,0},{16,24},{24,16},{1,9},{9,1},{17,25},{25,17},{2,10},{10... | collective-permute-start | bytes 589832 | tf_op jit(solution)/shard_map/ppermute | solution.py:23
  40.2 1.7 %fusion.3 = f32[3,8,16,128]{3,2,1,0:T(8,128)} fusion(f32[2,3,8,16,128]{4,3,2,1,0:T(8,128)S(1)} %collective-permute-done.20, f32[1,1,3,32,16,128]{5,4,3,2,1,0:T(8,128)} %get-tuple-element.29, s32[]{:T(128)S(6)} %select_n.65, pred[3]{0:T(512)(128)(4,1)S(1)} %get-tuple-element.48), kind=kLoop, calls=%fused_computation.14 | loop fusion | flops 49152 | bytes 589831 | tf_op jit(solution)/shard_map/jit(_where)/select_n | solution.py:49
  41.9 2.1 %collective-permute-done.4.refs_1_ = f32[3,8,16,128]{3,2,1,0:T(8,128)S(1)} collective-permute-done((f32[3,8,16,128]{3,2,1,0:T(8,128)S(1)}, f32[3,8,16,128]{3,2,1,0:T(8,128)S(1)}, u32[]{:S(2)}, u32[]{:S(2)}) %collective-permute-start.4) | collective-permute-done | bytes 196640 | tf_op jit(solution)/shard_map/ppermute | solution.py:23
  44.0 1.5 %collective-permute-start.1 = (f32[8,3,32,128]{3,2,1,0:T(8,128)}, f32[8,3,32,128]{3,2,1,0:T(8,128)S(1)}, u32[]{:S(2)}, u32[]{:S(2)}) collective-permute-start(f32[8,3,32,128]{3,2,1,0:T(8,128)} %bitcast.86), channel_id=1, source_target_pairs={{0,7},{1,0},{2,1},{3,2},{4,3},{5,4},{6,5},{7,6},{8,15},{9,8},{10,9... | collective-permute-start | bytes 1179656 | tf_op jit(solution)/shard_map/ppermute | solution.py:28
  45.5 2.7 %collective-permute-done.9.refs_5_ = f32[3,8,16,128]{3,2,1,0:T(8,128)S(1)} collective-permute-done((f32[3,8,16,128]{3,2,1,0:T(8,128)S(1)}, f32[3,8,16,128]{3,2,1,0:T(8,128)S(1)}, u32[]{:S(2)}, u32[]{:S(2)}) %collective-permute-start.9) | collective-permute-done | bytes 196640 | tf_op jit(solution)/shard_map/ppermute | solution.py:23
  49.1 1.6 %collective-permute-start.21 = (f32[3,8,16,128]{3,2,1,0:T(8,128)}, f32[3,8,16,128]{3,2,1,0:T(8,128)}, u32[]{:S(2)}, u32[]{:S(2)}) collective-permute-start(f32[3,8,16,128]{3,2,1,0:T(8,128)} %fusion.3), channel_id=1, source_target_pairs={{0,16},{8,24},{16,0},{24,8},{1,17},{9,25},{17,1},{25,9},{2,18},{10... | collective-permute-start | bytes 589832 | tf_op jit(solution)/shard_map/ppermute | solution.py:23
  50.7 1.7 %collective-permute-done.6.refs_3_ = f32[3,8,16,128]{3,2,1,0:T(8,128)S(1)} collective-permute-done((f32[3,8,16,128]{3,2,1,0:T(8,128)S(1)}, f32[3,8,16,128]{3,2,1,0:T(8,128)S(1)}, u32[]{:S(2)}, u32[]{:S(2)}) %collective-permute-start.6) | collective-permute-done | bytes 196640 | tf_op jit(solution)/shard_map/ppermute | solution.py:23
  53.0 5.5 %collective-permute-done.11.refs_7_ = f32[3,8,16,128]{3,2,1,0:T(8,128)S(1)} collective-permute-done((f32[3,8,16,128]{3,2,1,0:T(8,128)S(1)}, f32[3,8,16,128]{3,2,1,0:T(8,128)S(1)}, u32[]{:S(2)}, u32[]{:S(2)}) %collective-permute-start.11) | collective-permute-done | bytes 196640 | tf_op jit(solution)/shard_map/ppermute | solution.py:23
  59.9 1.6 %collective-permute-start.16 = (f32[9,32,128]{2,1,0:T(8,128)S(1)}, f32[9,32,128]{2,1,0:T(8,128)S(1)}, u32[]{:S(2)}, u32[]{:S(2)}) collective-permute-start(f32[9,32,128]{2,1,0:T(8,128)S(1)} %get-tuple-element.16), channel_id=1, source_target_pairs={{0,7},{1,0},{2,1},{3,2},{4,3},{5,4},{6,5},{7,6},{8,15},{9,8},{10,9... | collective-permute-start | bytes 442376 | tf_op jit(solution)/shard_map/ppermute | solution.py:28
  62.8 1.5 %collective-permute-start.22 = (f32[3,8,16,128]{3,2,1,0:T(8,128)S(1)}, f32[3,8,16,128]{3,2,1,0:T(8,128)S(1)}, u32[]{:S(2)}, u32[]{:S(2)}) collective-permute-start(f32[3,8,16,128]{3,2,1,0:T(8,128)S(1)} %get-tuple-element.43.refs_0_), channel_id=1, source_target_pairs={{0,8},{8,0},{16,24},{24,16},{1,9},{9,1},{17,25},{25,17},{2,10},{10... | collective-permute-start | bytes 589832 | tf_op jit(solution)/shard_map/ppermute | solution.py:23
  64.3 1.3 %collective-permute-start.23 = (f32[3,8,16,128]{3,2,1,0:T(8,128)S(1)}, f32[3,8,16,128]{3,2,1,0:T(8,128)S(1)}, u32[]{:S(2)}, u32[]{:S(2)}) collective-permute-start(f32[3,8,16,128]{3,2,1,0:T(8,128)S(1)} %get-tuple-element.43.refs_0_), channel_id=1, source_target_pairs={{0,16},{8,24},{16,0},{24,8},{1,17},{9,25},{17,1},{25,9},{2,18},{10... | collective-permute-start | bytes 589832 | tf_op jit(solution)/shard_map/ppermute | solution.py:23
  68.2 3.9 %collective-permute-done.17.rest_0_ = f32[6,32,128]{2,1,0:T(8,128)S(1)} collective-permute-done((f32[6,32,128]{2,1,0:T(8,128)S(1)}, f32[6,32,128]{2,1,0:T(8,128)S(1)}, u32[]{:S(2)}, u32[]{:S(2)}) %collective-permute-start.17) | collective-permute-done | bytes 98336 | tf_op jit(solution)/shard_map/ppermute | solution.py:28
  72.2 13.9 %steps_0.1 = (f32[8,16,32,128]{3,2,1,0:T(8,128)}, f32[8,3,32,128]{3,2,1,0:T(8,128)S(1)}, f32[8,3,32,128]{3,2,1,0:T(8,128)S(1)}, f32[8,16,128]{2,1,0:T(8,128)S(1)}) custom-call(s32[8]{0:T(128)S(1)} %copy-done.1, s32[8]{0:T(128)S(1)} %copy-done.2, s32[8]{0:T(128)S(1)} %copy-done.3, s32[1]{0:T(128)} %bitcast.start_ref, f32[8,32,16,128]{3,2,1,0:T(8,128)} %field_ref.1, ...), custom_call_target="tpu_custom_call" | custom-call | flops 301989888 | bytes 4194304 | tf_op jit(solution)/shard_map/steps_0/pallas_call | solution.py:266
  86.1 3.5 %collective-permute-start.19 = (f32[8,3,32,128]{3,2,1,0:T(8,128)S(1)}, f32[8,3,32,128]{3,2,1,0:T(8,128)S(1)}, u32[]{:S(2)}, u32[]{:S(2)}) collective-permute-start(f32[8,3,32,128]{3,2,1,0:T(8,128)S(1)} %get-tuple-element.20), channel_id=1, source_target_pairs={{0,7},{1,0},{2,1},{3,2},{4,3},{5,4},{6,5},{7,6},{8,15},{9,8},{10,9... | collective-permute-start | bytes 1179656 | tf_op jit(solution)/shard_map/ppermute | solution.py:28
  90.3 1.4 %collective-permute-start.24 = (f32[3,8,16,128]{3,2,1,0:T(8,128)S(1)}, f32[3,8,16,128]{3,2,1,0:T(8,128)S(1)}, u32[]{:S(2)}, u32[]{:S(2)}) collective-permute-start(f32[3,8,16,128]{3,2,1,0:T(8,128)S(1)} %collective-permute-done.23.refs_2_), channel_id=1, source_target_pairs={{0,8},{8,0},{16,24},{24,16},{1,9},{9,1},{17,25},{25,17},{2,10},{10... | collective-permute-start | bytes 589832 | tf_op jit(solution)/shard_map/ppermute | solution.py:23
  93.0 2.5 %collective-permute-done.28.refs_6_ = f32[3,8,16,128]{3,2,1,0:T(8,128)S(1)} collective-permute-done((f32[3,8,16,128]{3,2,1,0:T(8,128)S(1)}, f32[3,8,16,128]{3,2,1,0:T(8,128)S(1)}, u32[]{:S(2)}, u32[]{:S(2)}) %collective-permute-start.28) | collective-permute-done | bytes 196640 | tf_op jit(solution)/shard_map/ppermute | solution.py:23
  96.0 1.7 %collective-permute-done.29.refs_7_ = f32[3,8,16,128]{3,2,1,0:T(8,128)S(1)} collective-permute-done((f32[3,8,16,128]{3,2,1,0:T(8,128)S(1)}, f32[3,8,16,128]{3,2,1,0:T(8,128)S(1)}, u32[]{:S(2)}, u32[]{:S(2)}) %collective-permute-start.29) | collective-permute-done | bytes 196640 | tf_op jit(solution)/shard_map/ppermute | solution.py:23
  98.3 2.6 %collective-permute-start.30 = (f32[9,32,128]{2,1,0:T(8,128)S(1)}, f32[9,32,128]{2,1,0:T(8,128)S(1)}, u32[]{:S(2)}, u32[]{:S(2)}) collective-permute-start(f32[9,32,128]{2,1,0:T(8,128)S(1)} %get-tuple-element.24), channel_id=1, source_target_pairs={{0,7},{1,0},{2,1},{3,2},{4,3},{5,4},{6,5},{7,6},{8,15},{9,8},{10,9... | collective-permute-start | bytes 442376 | tf_op jit(solution)/shard_map/ppermute | solution.py:28
  101.8 5.0 %collective-permute-done.31.rest_0_ = f32[6,32,128]{2,1,0:T(8,128)S(1)} collective-permute-done((f32[6,32,128]{2,1,0:T(8,128)S(1)}, f32[6,32,128]{2,1,0:T(8,128)S(1)}, u32[]{:S(2)}, u32[]{:S(2)}) %collective-permute-start.31) | collective-permute-done | bytes 98336 | tf_op jit(solution)/shard_map/ppermute | solution.py:28
  106.8 13.1 %steps_3.1 = (f32[8,32,16,128]{3,2,1,0:T(8,128)}, f32[8,16,128]{2,1,0:T(8,128)}) custom-call(s32[8]{0:T(128)S(1)} %copy-done.1, s32[8]{0:T(128)S(1)} %copy-done.2, s32[8]{0:T(128)S(1)} %copy-done.3, s32[1]{0:T(128)} %bitcast.start_ref, f32[8,16,32,128]{3,2,1,0:T(8,128)S(1)} %copy-done, f32[8,3,32,128]{3,2,1,0:T(8,128)S(1)} %collective-permute-done.18.west_ref, ...), custom_call_target="tpu_custom_call" | custom-call | flops 301989888 | bytes 4194304 | tf_op jit(solution)/shard_map/steps_3/pallas_call | solution.py:266
  (97 shorter events, 23.8 us)
Async XLA Ops:
  5.6 12.6 %collective-permute-start.7 = (f32[2,3,8,16,128]{4,3,2,1,0:T(8,128)}, f32[2,3,8,16,128]{4,3,2,1,0:T(8,128)}, u32[]{:S(2)}, u32[]{:S(2)}) collective-permute-start(f32[2,3,8,16,128]{4,3,2,1,0:T(8,128)} %pad_maximum_fusion.1), channel_id=1, source_target_pairs={{0,16},{8,24},{16,0},{24,8},{1,17},{9,25},{17,1},{25,9},{2,18},{10... | collective-permute-start | bytes 1179656 | tf_op jit(solution)/shard_map/ppermute | solution.py:23
  10.4 11.8 %collective-permute-start.2 = (f32[2,3,8,16,128]{4,3,2,1,0:T(8,128)}, f32[2,3,8,16,128]{4,3,2,1,0:T(8,128)}, u32[]{:S(2)}, u32[]{:S(2)}) collective-permute-start(f32[2,3,8,16,128]{4,3,2,1,0:T(8,128)} %pad_maximum_fusion), channel_id=1, source_target_pairs={{0,8},{8,0},{16,24},{24,16},{1,9},{9,1},{17,25},{25,17},{2,10},{10... | collective-permute-start | bytes 1179656 | tf_op jit(solution)/shard_map/ppermute | solution.py:23
  12.9 14.9 %collective-permute-start.13 = (f32[1,32,128]{2,1,0:T(8,128)S(1)}, f32[1,32,128]{2,1,0:T(8,128)S(1)}, u32[]{:S(2)}, u32[]{:S(2)}) collective-permute-start(f32[1,32,128]{2,1,0:T(8,128)S(1)} %slice.94), channel_id=1, source_target_pairs={{0,7},{1,0},{2,1},{3,2},{4,3},{5,4},{6,5},{7,6},{8,15},{9,8},{10,9... | collective-permute-start | bytes 49160 | tf_op jit(solution)/shard_map/ppermute | solution.py:28
  15.5 12.3 %collective-permute-start.12 = (f32[1,32,128]{2,1,0:T(8,128)S(1)}, f32[1,32,128]{2,1,0:T(8,128)S(1)}, u32[]{:S(2)}, u32[]{:S(2)}) collective-permute-start(f32[1,32,128]{2,1,0:T(8,128)S(1)} %slice.92), channel_id=1, source_target_pairs={{0,1},{1,2},{2,3},{3,4},{4,5},{5,6},{6,7},{7,0},{8,9},{9,10},{10,1... | collective-permute-start | bytes 49160 | tf_op jit(solution)/shard_map/ppermute | solution.py:28
  16.4 17.5 %collective-permute-start.25 = (f32[2,3,8,16,128]{4,3,2,1,0:T(8,128)}, f32[2,3,8,16,128]{4,3,2,1,0:T(8,128)}, u32[]{:S(2)}, u32[]{:S(2)}) collective-permute-start(f32[2,3,8,16,128]{4,3,2,1,0:T(8,128)} %pad_maximum_fusion.4), channel_id=1, source_target_pairs={{0,16},{8,24},{16,0},{24,8},{1,17},{9,25},{17,1},{25,9},{2,18},{10... | collective-permute-start | bytes 1179656 | tf_op jit(solution)/shard_map/ppermute | solution.py:23
  20.1 9.8 %collective-permute-start.8 = (f32[3,8,16,128]{3,2,1,0:T(8,128)}, f32[3,8,16,128]{3,2,1,0:T(8,128)S(1)}, u32[]{:S(2)}, u32[]{:S(2)}) collective-permute-start(f32[3,8,16,128]{3,2,1,0:T(8,128)} %fusion.6), channel_id=1, source_target_pairs={{0,8},{8,0},{16,24},{24,16},{1,9},{9,1},{17,25},{25,17},{2,10},{10... | collective-permute-start | bytes 589832 | tf_op jit(solution)/shard_map/ppermute | solution.py:23
  24.0 7.2 %collective-permute-start.3 = (f32[3,8,16,128]{3,2,1,0:T(8,128)}, f32[3,8,16,128]{3,2,1,0:T(8,128)}, u32[]{:S(2)}, u32[]{:S(2)}) collective-permute-start(f32[3,8,16,128]{3,2,1,0:T(8,128)} %fusion.9), channel_id=1, source_target_pairs={{0,16},{8,24},{16,0},{24,8},{1,17},{9,25},{17,1},{25,9},{2,18},{10... | collective-permute-start | bytes 589832 | tf_op jit(solution)/shard_map/ppermute | solution.py:23
  27.8 9.9 %collective-permute-start.20 = (f32[2,3,8,16,128]{4,3,2,1,0:T(8,128)S(1)}, f32[2,3,8,16,128]{4,3,2,1,0:T(8,128)S(1)}, u32[]{:S(2)}, u32[]{:S(2)}) collective-permute-start(f32[2,3,8,16,128]{4,3,2,1,0:T(8,128)S(1)} %pad_maximum_fusion.3), channel_id=1, source_target_pairs={{0,8},{8,0},{16,24},{24,16},{1,9},{9,1},{17,25},{25,17},{2,10},{10... | collective-permute-start | bytes 1179656 | tf_op jit(solution)/shard_map/ppermute | solution.py:23
  27.8 14.1 %collective-permute-start.14 = (f32[1,6,32,128]{3,2,1,0:T(8,128)S(1)}, f32[1,6,32,128]{3,2,1,0:T(8,128)S(1)}, u32[]{:S(2)}, u32[]{:S(2)}) collective-permute-start(f32[1,6,32,128]{3,2,1,0:T(8,128)S(1)} %maximum_bitcast_fusion), channel_id=1, source_target_pairs={{0,8},{8,0},{16,24},{24,16},{1,9},{9,1},{17,25},{25,17},{2,10},{10... | collective-permute-start | bytes 294920 | tf_op jit(solution)/shard_map/ppermute | solution.py:23
  32.6 5.9 %collective-permute-start.5 = (f32[3,8,16,128]{3,2,1,0:T(8,128)S(1)}, f32[3,8,16,128]{3,2,1,0:T(8,128)S(1)}, u32[]{:S(2)}, u32[]{:S(2)}) collective-permute-start(f32[3,8,16,128]{3,2,1,0:T(8,128)S(1)} %get-tuple-element.45.refs_0_), channel_id=1, source_target_pairs={{0,16},{8,24},{16,0},{24,8},{1,17},{9,25},{17,1},{25,9},{2,18},{10... | collective-permute-start | bytes 589832 | tf_op jit(solution)/shard_map/ppermute | solution.py:23
  35.6 8.4 %collective-permute-start.4 = (f32[3,8,16,128]{3,2,1,0:T(8,128)S(1)}, f32[3,8,16,128]{3,2,1,0:T(8,128)S(1)}, u32[]{:S(2)}, u32[]{:S(2)}) collective-permute-start(f32[3,8,16,128]{3,2,1,0:T(8,128)S(1)} %get-tuple-element.45.refs_0_), channel_id=1, source_target_pairs={{0,8},{8,0},{16,24},{24,16},{1,9},{9,1},{17,25},{25,17},{2,10},{10... | collective-permute-start | bytes 589832 | tf_op jit(solution)/shard_map/ppermute | solution.py:23
  37.1 11.1 %collective-permute-start.9 = (f32[3,8,16,128]{3,2,1,0:T(8,128)S(1)}, f32[3,8,16,128]{3,2,1,0:T(8,128)S(1)}, u32[]{:S(2)}, u32[]{:S(2)}) collective-permute-start(f32[3,8,16,128]{3,2,1,0:T(8,128)S(1)} %get-tuple-element.44.refs_4_), channel_id=1, source_target_pairs={{0,8},{8,0},{16,24},{24,16},{1,9},{9,1},{17,25},{25,17},{2,10},{10... | collective-permute-start | bytes 589832 | tf_op jit(solution)/shard_map/ppermute | solution.py:23
  37.7 11.4 %collective-permute-start.10 = (f32[3,8,16,128]{3,2,1,0:T(8,128)S(1)}, f32[3,8,16,128]{3,2,1,0:T(8,128)S(1)}, u32[]{:S(2)}, u32[]{:S(2)}) collective-permute-start(f32[3,8,16,128]{3,2,1,0:T(8,128)S(1)} %get-tuple-element.44.refs_4_), channel_id=1, source_target_pairs={{0,16},{8,24},{16,0},{24,8},{1,17},{9,25},{17,1},{25,9},{2,18},{10... | collective-permute-start | bytes 589832 | tf_op jit(solution)/shard_map/ppermute | solution.py:23
  38.5 13.9 %collective-permute-start.6 = (f32[3,8,16,128]{3,2,1,0:T(8,128)S(1)}, f32[3,8,16,128]{3,2,1,0:T(8,128)S(1)}, u32[]{:S(2)}, u32[]{:S(2)}) collective-permute-start(f32[3,8,16,128]{3,2,1,0:T(8,128)S(1)} %collective-permute-done.5.refs_2_), channel_id=1, source_target_pairs={{0,8},{8,0},{16,24},{24,16},{1,9},{9,1},{17,25},{25,17},{2,10},{10... | collective-permute-start | bytes 589832 | tf_op jit(solution)/shard_map/ppermute | solution.py:23
  41.9 23.7 %collective-permute-start = (f32[8,3,32,128]{3,2,1,0:T(8,128)}, f32[8,3,32,128]{3,2,1,0:T(8,128)S(1)}, u32[]{:S(2)}, u32[]{:S(2)}) collective-permute-start(f32[8,3,32,128]{3,2,1,0:T(8,128)} %bitcast.87), channel_id=1, source_target_pairs={{0,1},{1,2},{2,3},{3,4},{4,5},{5,6},{6,7},{7,0},{8,9},{9,10},{10,1... | collective-permute-start | bytes 1179656 | tf_op jit(solution)/shard_map/ppermute | solution.py:28
  44.0 22.3 %collective-permute-start.1 = (f32[8,3,32,128]{3,2,1,0:T(8,128)}, f32[8,3,32,128]{3,2,1,0:T(8,128)S(1)}, u32[]{:S(2)}, u32[]{:S(2)}) collective-permute-start(f32[8,3,32,128]{3,2,1,0:T(8,128)} %bitcast.86), channel_id=1, source_target_pairs={{0,7},{1,0},{2,1},{3,2},{4,3},{5,4},{6,5},{7,6},{8,15},{9,8},{10,9... | collective-permute-start | bytes 1179656 | tf_op jit(solution)/shard_map/ppermute | solution.py:28
  48.2 11.7 %collective-permute-start.26 = (f32[3,8,16,128]{3,2,1,0:T(8,128)}, f32[3,8,16,128]{3,2,1,0:T(8,128)S(1)}, u32[]{:S(2)}, u32[]{:S(2)}) collective-permute-start(f32[3,8,16,128]{3,2,1,0:T(8,128)} %fusion), channel_id=1, source_target_pairs={{0,8},{8,0},{16,24},{24,16},{1,9},{9,1},{17,25},{25,17},{2,10},{10... | collective-permute-start | bytes 589832 | tf_op jit(solution)/shard_map/ppermute | solution.py:23
  49.1 12.4 %collective-permute-start.21 = (f32[3,8,16,128]{3,2,1,0:T(8,128)}, f32[3,8,16,128]{3,2,1,0:T(8,128)}, u32[]{:S(2)}, u32[]{:S(2)}) collective-permute-start(f32[3,8,16,128]{3,2,1,0:T(8,128)} %fusion.3), channel_id=1, source_target_pairs={{0,16},{8,24},{16,0},{24,8},{1,17},{9,25},{17,1},{25,9},{2,18},{10... | collective-permute-start | bytes 589832 | tf_op jit(solution)/shard_map/ppermute | solution.py:23
  52.4 6.1 %collective-permute-start.11 = (f32[3,8,16,128]{3,2,1,0:T(8,128)S(1)}, f32[3,8,16,128]{3,2,1,0:T(8,128)S(1)}, u32[]{:S(2)}, u32[]{:S(2)}) collective-permute-start(f32[3,8,16,128]{3,2,1,0:T(8,128)S(1)} %collective-permute-done.9.refs_5_), channel_id=1, source_target_pairs={{0,16},{8,24},{16,0},{24,8},{1,17},{9,25},{17,1},{25,9},{2,18},{10... | collective-permute-start | bytes 589832 | tf_op jit(solution)/shard_map/ppermute | solution.py:23
  58.5 5.8 %collective-permute-start.15 = (f32[2,6,32,128]{3,2,1,0:T(8,128)S(1)}, f32[2,6,32,128]{3,2,1,0:T(8,128)S(1)}, u32[]{:S(2)}, u32[]{:S(2)}) collective-permute-start(f32[2,6,32,128]{3,2,1,0:T(8,128)S(1)} %pad_maximum_fusion.5), channel_id=1, source_target_pairs={{0,16},{8,24},{16,0},{24,8},{1,17},{9,25},{17,1},{25,9},{2,18},{10... | collective-permute-start | bytes 589832 | tf_op jit(solution)/shard_map/ppermute | solution.py:23
  59.9 12.2 %collective-permute-start.16 = (f32[9,32,128]{2,1,0:T(8,128)S(1)}, f32[9,32,128]{2,1,0:T(8,128)S(1)}, u32[]{:S(2)}, u32[]{:S(2)}) collective-permute-start(f32[9,32,128]{2,1,0:T(8,128)S(1)} %get-tuple-element.16), channel_id=1, source_target_pairs={{0,7},{1,0},{2,1},{3,2},{4,3},{5,4},{6,5},{7,6},{8,15},{9,8},{10,9... | collective-permute-start | bytes 442376 | tf_op jit(solution)/shard_map/ppermute | solution.py:28
  62.8 26.9 %collective-permute-start.22 = (f32[3,8,16,128]{3,2,1,0:T(8,128)S(1)}, f32[3,8,16,128]{3,2,1,0:T(8,128)S(1)}, u32[]{:S(2)}, u32[]{:S(2)}) collective-permute-start(f32[3,8,16,128]{3,2,1,0:T(8,128)S(1)} %get-tuple-element.43.refs_0_), channel_id=1, source_target_pairs={{0,8},{8,0},{16,24},{24,16},{1,9},{9,1},{17,25},{25,17},{2,10},{10... | collective-permute-start | bytes 589832 | tf_op jit(solution)/shard_map/ppermute | solution.py:23
  64.3 26.0 %collective-permute-start.23 = (f32[3,8,16,128]{3,2,1,0:T(8,128)S(1)}, f32[3,8,16,128]{3,2,1,0:T(8,128)S(1)}, u32[]{:S(2)}, u32[]{:S(2)}) collective-permute-start(f32[3,8,16,128]{3,2,1,0:T(8,128)S(1)} %get-tuple-element.43.refs_0_), channel_id=1, source_target_pairs={{0,16},{8,24},{16,0},{24,8},{1,17},{9,25},{17,1},{25,9},{2,18},{10... | collective-permute-start | bytes 589832 | tf_op jit(solution)/shard_map/ppermute | solution.py:23
  65.6 26.1 %collective-permute-start.27 = (f32[3,8,16,128]{3,2,1,0:T(8,128)S(1)}, f32[3,8,16,128]{3,2,1,0:T(8,128)S(1)}, u32[]{:S(2)}, u32[]{:S(2)}) collective-permute-start(f32[3,8,16,128]{3,2,1,0:T(8,128)S(1)} %get-tuple-element.42.refs_4_), channel_id=1, source_target_pairs={{0,8},{8,0},{16,24},{24,16},{1,9},{9,1},{17,25},{25,17},{2,10},{10... | collective-permute-start | bytes 589832 | tf_op jit(solution)/shard_map/ppermute | solution.py:23
  66.3 5.8 %collective-permute-start.17 = (f32[6,32,128]{2,1,0:T(8,128)S(1)}, f32[6,32,128]{2,1,0:T(8,128)S(1)}, u32[]{:S(2)}, u32[]{:S(2)}) collective-permute-start(f32[6,32,128]{2,1,0:T(8,128)S(1)} %get-tuple-element.17), channel_id=1, source_target_pairs={{0,1},{1,2},{2,3},{3,4},{4,5},{5,6},{6,7},{7,0},{8,9},{9,10},{10,1... | collective-permute-start | bytes 294920 | tf_op jit(solution)/shard_map/ppermute | solution.py:28
  86.1 20.7 %collective-permute-start.18 = (f32[8,3,32,128]{3,2,1,0:T(8,128)S(1)}, f32[8,3,32,128]{3,2,1,0:T(8,128)S(1)}, u32[]{:S(2)}, u32[]{:S(2)}) collective-permute-start(f32[8,3,32,128]{3,2,1,0:T(8,128)S(1)} %get-tuple-element.19), channel_id=1, source_target_pairs={{0,1},{1,2},{2,3},{3,4},{4,5},{5,6},{6,7},{7,0},{8,9},{9,10},{10,1... | collective-permute-start | bytes 1179656 | tf_op jit(solution)/shard_map/ppermute | solution.py:28
  86.1 20.7 %collective-permute-start.19 = (f32[8,3,32,128]{3,2,1,0:T(8,128)S(1)}, f32[8,3,32,128]{3,2,1,0:T(8,128)S(1)}, u32[]{:S(2)}, u32[]{:S(2)}) collective-permute-start(f32[8,3,32,128]{3,2,1,0:T(8,128)S(1)} %get-tuple-element.20), channel_id=1, source_target_pairs={{0,7},{1,0},{2,1},{3,2},{4,3},{5,4},{6,5},{7,6},{8,15},{9,8},{10,9... | collective-permute-start | bytes 1179656 | tf_op jit(solution)/shard_map/ppermute | solution.py:28
  89.7 5.9 %collective-permute-start.28 = (f32[3,8,16,128]{3,2,1,0:T(8,128)S(1)}, f32[3,8,16,128]{3,2,1,0:T(8,128)S(1)}, u32[]{:S(2)}, u32[]{:S(2)}) collective-permute-start(f32[3,8,16,128]{3,2,1,0:T(8,128)S(1)} %get-tuple-element.42.refs_4_), channel_id=1, source_target_pairs={{0,16},{8,24},{16,0},{24,8},{1,17},{9,25},{17,1},{25,9},{2,18},{10... | collective-permute-start | bytes 589832 | tf_op jit(solution)/shard_map/ppermute | solution.py:23
  90.3 5.7 %collective-permute-start.24 = (f32[3,8,16,128]{3,2,1,0:T(8,128)S(1)}, f32[3,8,16,128]{3,2,1,0:T(8,128)S(1)}, u32[]{:S(2)}, u32[]{:S(2)}) collective-permute-start(f32[3,8,16,128]{3,2,1,0:T(8,128)S(1)} %collective-permute-done.23.refs_2_), channel_id=1, source_target_pairs={{0,8},{8,0},{16,24},{24,16},{1,9},{9,1},{17,25},{25,17},{2,10},{10... | collective-permute-start | bytes 589832 | tf_op jit(solution)/shard_map/ppermute | solution.py:23
  91.7 5.9 %collective-permute-start.29 = (f32[3,8,16,128]{3,2,1,0:T(8,128)S(1)}, f32[3,8,16,128]{3,2,1,0:T(8,128)S(1)}, u32[]{:S(2)}, u32[]{:S(2)}) collective-permute-start(f32[3,8,16,128]{3,2,1,0:T(8,128)S(1)} %collective-permute-done.27.refs_5_), channel_id=1, source_target_pairs={{0,16},{8,24},{16,0},{24,8},{1,17},{9,25},{17,1},{25,9},{2,18},{10... | collective-permute-start | bytes 589832 | tf_op jit(solution)/shard_map/ppermute | solution.py:23
  98.3 8.5 %collective-permute-start.30 = (f32[9,32,128]{2,1,0:T(8,128)S(1)}, f32[9,32,128]{2,1,0:T(8,128)S(1)}, u32[]{:S(2)}, u32[]{:S(2)}) collective-permute-start(f32[9,32,128]{2,1,0:T(8,128)S(1)} %get-tuple-element.24), channel_id=1, source_target_pairs={{0,7},{1,0},{2,1},{3,2},{4,3},{5,4},{6,5},{7,6},{8,15},{9,8},{10,9... | collective-permute-start | bytes 442376 | tf_op jit(solution)/shard_map/ppermute | solution.py:28
  101.0 5.8 %collective-permute-start.31 = (f32[6,32,128]{2,1,0:T(8,128)S(1)}, f32[6,32,128]{2,1,0:T(8,128)S(1)}, u32[]{:S(2)}, u32[]{:S(2)}) collective-permute-start(f32[6,32,128]{2,1,0:T(8,128)S(1)} %get-tuple-element.25), channel_id=1, source_target_pairs={{0,1},{1,2},{2,3},{3,4},{4,5},{5,6},{6,7},{7,0},{8,9},{9,10},{10,1... | collective-permute-start | bytes 294920 | tf_op jit(solution)/shard_map/ppermute | solution.py:28
  (14 other events, 105.7 us)
